TPU v7x, 512 devices: a whole 4x4x16 slice. The times are simulated.
512 devices in a mesh: section: 16 (over z), expert: 32 (over x, y, core).
Axes of the slice: x: 4, y: 4, z: 16, core: 2. Of those that a mesh axis runs over, the one named last changes fastest.
Arguments:
- section_in: bfloat16 [16, 1024, 2048], P('section', 'expert'), may hold values from -6 to 6
- new_batch: bfloat16 [1, 1024, 2048], P(None, 'expert'), may hold values from -6 to 6
- stashed: bfloat16 [2, 16, 1024, 2048], P(None, 'section', 'expert'), may hold values from -6 to 6
- grad_in: bfloat16 [16, 1024, 2048], P('section', 'expert'), may hold values from -6 to 6
- loss_grad: bfloat16 [1, 1024, 2048], P(None, 'expert'), may hold values from -6 to 6
- routes: int32 [2, 2, 16, 1024, 2], P(None, None, 'section', 'expert'), may hold values from 0 to 7, all different within a row; in each aligned block of 32 rows (0 to 31, 32 to 63, ..., all dimensions but the last counted through in order) at most 8 rows name the same one
- counts: int32 [2, 2, 16, 1024], P(None, None, 'section', 'expert'), may hold values from 0 to 2, as said below
- norm_gain: float32 [16, 2048], P('section'), may hold values from 0.1 to 1.9
- w_router: bfloat16 [16, 2048, 8], P('section'), may hold values from -0.125 to 0.125
- w_gate: bfloat16 [16, 2048, 8192], P('section', None, 'expert'), may hold values from -0.125 to 0.125
- w_up: bfloat16 [16, 2048, 8192], P('section', None, 'expert'), may hold values from -0.125 to 0.125
- w_down: bfloat16 [16, 8192, 2048], P('section', 'expert'), may hold values from -0.1875 to 0.1875
- lam: float32 [16], P('section'), may hold values from 4 to 40
Outputs:
- fwd_out: bfloat16 [2, 16, 1024, 2048], P(None, 'section', 'expert')
- grad_out: bfloat16 [2, 16, 1024, 2048], P(None, 'section', 'expert')
- lam_out: float32 [16], P('section')
Inputs may be any that keep to these rules, and one draw needn't show every extreme that they name: routes[m, k, s, t] names 2 different experts; among the 32 tokens of one device's aligned block no expert is named more than 8 times. counts[m, k, s, t] active entries come first in the token's list.
All inputs are finite; a program needn't handle non-finite values.
Results may differ from a plain program's by a relative error of at most 0.01.
Values may be sent and summed in bfloat16 or wider, within the bound.
A program may use at most 128 MiB of HBM per device.

v0:
```python
import jax
import jax.numpy as jnp
from jax import lax
from jax.sharding import PartitionSpec as P

SPLIT = 4
TICKS = 2


def shortened(value):

    def short(part):
        return part.astype(jnp.bfloat16) if part.dtype == jnp.float32 else part

    return jax.tree.map(short, value)


def from_behind(block, axis, distance):
    devices = range(lax.axis_size(axis))
    route = [(i - distance, i) for i in devices if i - distance in devices]
    return lax.ppermute(block, axis, route)


def norm_rows(values, gain_row):
    return values * lax.rsqrt(jnp.mean(values * values, axis=-1, keepdims=True) + 1e-05) * gain_row


def quarter_work(rows_f, rows_b, grads, scales, gate_q, up_q, down_q):
    all_rows = jnp.concatenate([rows_f, rows_b], axis=0)
    pre_gate = jnp.dot(all_rows, gate_q, preferred_element_type=jnp.float32)
    pre_up = jnp.dot(all_rows, up_q, preferred_element_type=jnp.float32)
    activated = jax.nn.silu(pre_gate)
    hidden = (activated * pre_up).astype(jnp.bfloat16)
    projected = jnp.dot(hidden, down_q, preferred_element_type=jnp.float32).astype(jnp.bfloat16)
    half_rows = rows_f.shape[0]
    scaled = (scales.astype(jnp.float32)[:, None] * grads.astype(jnp.float32)).astype(jnp.bfloat16)
    back_h = jnp.dot(scaled, down_q.T, preferred_element_type=jnp.float32)
    gate_tail = pre_gate[half_rows:]
    sigmoid_g = jax.nn.sigmoid(gate_tail)
    silu_slope = sigmoid_g * (1.0 + gate_tail * (1.0 - sigmoid_g))
    d_gate = (back_h * pre_up[half_rows:] * silu_slope).astype(jnp.bfloat16)
    d_up = (back_h * activated[half_rows:]).astype(jnp.bfloat16)
    d_rows = (
        jnp.dot(d_gate, gate_q.T, preferred_element_type=jnp.float32)
        + jnp.dot(d_up, up_q.T, preferred_element_type=jnp.float32)
    ).astype(jnp.bfloat16)
    inner_dot = jnp.sum(
        grads.astype(jnp.float32) * projected[half_rows:].astype(jnp.float32), axis=-1
    ).astype(jnp.bfloat16)
    return (projected[:half_rows], d_rows, inner_dot)


def slot_tables(route, count, experts, capacity):
    tok_rows, top_slots = route.shape
    flat_list = route.reshape(tok_rows * top_slots)
    onehot = (flat_list[:, None] == jnp.arange(experts, dtype=jnp.int32)[None, :]).astype(jnp.int32)
    slot_rank = jnp.sum((jnp.cumsum(onehot, axis=0) - 1) * onehot, axis=1)
    target = (flat_list * capacity + slot_rank).reshape(tok_rows, top_slots)
    live_mask = jnp.arange(top_slots, dtype=jnp.int32)[None, :] < count[:, None]
    slot_table = (
        (target[:, :, None] == jnp.arange(experts * capacity, dtype=jnp.int32)[None, None, :])
        & live_mask[:, :, None]
    ).astype(jnp.bfloat16)
    return (slot_table, target, live_mask.astype(jnp.float32))


def route_rows(rows_f, rows_b, grads_b, scales_b, experts, capacity, gate_cols, up_cols, down_rows):
    width = rows_f.shape[-1]

    def work(got_f, got_b, got_g, got_s):
        leading = got_f.shape[:-1]
        projected, d_rows, inner_dot = quarter_work(
            got_f.reshape(-1, width),
            got_b.reshape(-1, width),
            got_g.reshape(-1, width),
            got_s.reshape(-1),
            gate_cols,
            up_cols,
            down_rows,
        )
        return (
            projected.reshape(leading + (width,)),
            d_rows.reshape(leading + (width,)),
            inner_dot.reshape(leading),
        )

    grouped_rows = (
        rows_f.reshape((experts, capacity, width)),
        rows_b.reshape((experts, capacity, width)),
        grads_b.reshape((experts, capacity, width)),
        scales_b.reshape((experts, capacity)),
    )
    outgoing = tuple(
        (
            jnp.broadcast_to(
                element.reshape((experts, 1) + element.shape[1:]),
                (experts, SPLIT) + element.shape[1:],
            ).reshape((experts * SPLIT,) + element.shape[1:])
            for element in grouped_rows
        )
    )
    received = jax.tree.map(
        lambda part, own: part.astype(own.dtype),
        lax.all_to_all(shortened(outgoing), "expert", split_axis=0, concat_axis=0, tiled=True),
        outgoing,
    )
    returned = lax.all_to_all(
        shortened(work(*received)), "expert", split_axis=0, concat_axis=0, tiled=True
    )
    return tuple(
        (
            jnp.sum(
                element.astype(jnp.float32).reshape((experts, SPLIT, capacity) + element.shape[2:]),
                axis=1,
            ).reshape((experts * capacity,) + element.shape[2:])
            for element in returned
        )
    )


def on_device(
    section_in,
    new_batch,
    stashed,
    grad_in,
    loss_grad,
    routes,
    counts,
    norm_gain,
    w_router,
    w_gate,
    w_up,
    w_down,
    lam,
):
    section_pos = lax.axis_index("section")
    last_section = lax.axis_size("section") - 1
    tok_rows = section_in.shape[1]
    top_slots = routes.shape[-1]
    experts = w_router.shape[-1]
    capacity = SPLIT * min(
        tok_rows // (2 * SPLIT), 5 * tok_rows * top_slots // (4 * experts * SPLIT)
    )
    share_total = tok_rows * lax.axis_size("expert") * top_slots
    gain_row = norm_gain[0]
    router = w_router[0]
    gate_cols = w_gate[0]
    up_cols = w_up[0]
    down_rows = w_down[0]
    totals = lax.psum(jnp.sum(counts[0, :, 0], axis=-1).astype(jnp.float32), "expert")
    weight = lam[0]
    forward_x = section_in[0]
    cotangent = grad_in[0]
    fwd_list = []
    grad_list = []
    for tick_num in range(TICKS):
        if tick_num > 0:
            arriving = from_behind(fwd_list[-1], "section", 1)
            forward_x = jnp.where(section_pos == 0, new_batch[tick_num - 1], arriving)
            coming = from_behind(grad_list[-1], "section", -1)
            cotangent = jnp.where(section_pos == last_section, loss_grad[tick_num - 1], coming)
        route_f = routes[0, tick_num, 0]
        route_b = routes[1, tick_num, 0]
        table_f, target_f, live_f = slot_tables(route_f, counts[0, tick_num, 0], experts, capacity)
        table_b, target_b, live_b = slot_tables(route_b, counts[1, tick_num, 0], experts, capacity)
        normed_f = norm_rows(forward_x.astype(jnp.float32), gain_row).astype(jnp.bfloat16)
        picked_f = jnp.take_along_axis(
            jnp.dot(normed_f, router, preferred_element_type=jnp.float32), route_f, axis=1
        )
        gate_f = jax.nn.softplus(picked_f) * live_f
        normed_raw, pullback = jax.vjp(
            lambda values: norm_rows(values, gain_row), stashed[tick_num, 0].astype(jnp.float32)
        )
        normed_b = normed_raw.astype(jnp.bfloat16)
        picked_b = jnp.take_along_axis(
            jnp.dot(normed_b, router, preferred_element_type=jnp.float32), route_b, axis=1
        )
        gate_b = jax.nn.softplus(picked_b) * live_b
        rows_f = jnp.einsum(
            "tjc,td->cd", table_f, normed_f, preferred_element_type=jnp.float32
        ).astype(jnp.bfloat16)
        rows_b = jnp.einsum(
            "tjc,td->cd", table_b, normed_b, preferred_element_type=jnp.float32
        ).astype(jnp.bfloat16)
        grads_b = jnp.einsum(
            "tjc,td->cd", table_b, cotangent, preferred_element_type=jnp.float32
        ).astype(jnp.bfloat16)
        scales_b = (
            jnp.zeros((experts * capacity,), jnp.float32)
            .at[target_b.reshape(-1)]
            .add(gate_b.reshape(-1))
            .astype(jnp.bfloat16)
        )
        y_slots, dn_slots, dot_slots = route_rows(
            rows_f, rows_b, grads_b, scales_b, experts, capacity, gate_cols, up_cols, down_rows
        )
        y_tok = jnp.take(y_slots, target_f, axis=0)
        out_f = (
            forward_x.astype(jnp.float32) + jnp.sum(gate_f[:, :, None] * y_tok, axis=1)
        ).astype(jnp.bfloat16)
        dpick = (jnp.take(dot_slots, target_b, axis=0) + weight) * jax.nn.sigmoid(picked_b) * live_b
        onehot_b = (
            route_b[:, :, None] == jnp.arange(experts, dtype=jnp.int32)[None, None, :]
        ).astype(jnp.float32)
        dlogit = jnp.sum(onehot_b * dpick[:, :, None], axis=1)
        dnorm = jnp.sum(
            live_b[:, :, None] * jnp.take(dn_slots, target_b, axis=0), axis=1
        ) + jnp.dot(dlogit, router.astype(jnp.float32).T, precision=lax.Precision.HIGHEST)
        grad_x = (cotangent.astype(jnp.float32) + pullback(dnorm)[0]).astype(jnp.bfloat16)
        fwd_list.append(out_f)
        grad_list.append(grad_x)
        weight = weight * jnp.exp(4.0 * (totals[tick_num] / share_total - 0.5))
    return (jnp.stack(fwd_list)[:, None], jnp.stack(grad_list)[:, None], weight.reshape(1))


def solution(mesh):
    in_specs = (
        P("section", "expert", None),
        P(None, "expert", None),
        P(None, "section", "expert", None),
        P("section", "expert", None),
        P(None, "expert", None),
        P(None, None, "section", "expert", None),
        P(None, None, "section", "expert"),
        P("section", None),
        P("section", None, None),
        P("section", None, "expert"),
        P("section", None, "expert"),
        P("section", "expert", None),
        P("section"),
    )
    out_specs = (
        P(None, "section", "expert", None),
        P(None, "section", "expert", None),
        P("section"),
    )
    return jax.shard_map(
        on_device, mesh=mesh, in_specs=in_specs, out_specs=out_specs, check_vma=False
    )
```

profile of v0, /device:TPU:1, one launch (start us, length us, event | category | flops | bytes accessed | tf_op | source)
XLA Modules:
  0.0 372.0 jit_solution(5309016546662161397)
XLA Ops:
  10.8 10.5 %all-to-all-start.1 = ((bf16[32,8,2048]{2,1,0:T(8,128)(2,1)}), bf16[32,8,2048]{2,1,0:T(8,128)(2,1)S(1)}, u32[]{:S(2)}, u32[]{:S(2)}) async-start(bf16[32,8,2048]{2,1,0:T(8,128)(2,1)} %bitcast.14), calls=%async_computation.1 | async-start | bytes 2097152 | tf_op jit(solution)/shard_map/all_to_all | solution.py:104
  25.6 12.6 %all-to-all-done.1 = bf16[32,8,2048]{2,1,0:T(8,128)(2,1)S(1)} async-done(((bf16[32,8,2048]{2,1,0:T(8,128)(2,1)}), bf16[32,8,2048]{2,1,0:T(8,128)(2,1)S(1)}, u32[]{:S(2)}, u32[]{:S(2)}) %all-to-all-start.1) | async-done | bytes 1048608 | tf_op jit(solution)/shard_map/all_to_all | solution.py:104
  39.5 4.4 %all-to-all-start = ((bf16[32,8,2048]{2,1,0:T(8,128)(2,1)}), bf16[32,8,2048]{2,1,0:T(8,128)(2,1)}, u32[]{:S(2)}, u32[]{:S(2)}) async-start(bf16[32,8,2048]{2,1,0:T(8,128)(2,1)} %bitcast.8), calls=%async_computation | async-start | bytes 2097152 | tf_op jit(solution)/shard_map/all_to_all | solution.py:104
  44.0 1.5 slice_reduce_fusion
  48.6 12.3 %all-to-all-done = bf16[32,8,2048]{2,1,0:T(8,128)(2,1)} async-done(((bf16[32,8,2048]{2,1,0:T(8,128)(2,1)}), bf16[32,8,2048]{2,1,0:T(8,128)(2,1)}, u32[]{:S(2)}, u32[]{:S(2)}) %all-to-all-start) | async-done | bytes 1048608 | tf_op jit(solution)/shard_map/all_to_all | solution.py:104
  62.1 3.9 %all-to-all-start.7 = ((bf16[32,8,2048]{2,1,0:T(8,128)(2,1)}), bf16[32,8,2048]{2,1,0:T(8,128)(2,1)S(1)}, u32[]{:S(2)}, u32[]{:S(2)}) async-start(bf16[32,8,2048]{2,1,0:T(8,128)(2,1)} %bitcast.50), calls=%async_computation.7 | async-start | bytes 2097152 | tf_op jit(solution)/shard_map/all_to_all | solution.py:104
  69.9 2.4 fusion.20
  72.3 2.9 divide_multiply_fusion.1
  75.3 2.1 convolution_convert_fusion.1
  77.4 5.6 %all-to-all-done.7 = bf16[32,8,2048]{2,1,0:T(8,128)(2,1)S(1)} async-done(((bf16[32,8,2048]{2,1,0:T(8,128)(2,1)}), bf16[32,8,2048]{2,1,0:T(8,128)(2,1)S(1)}, u32[]{:S(2)}, u32[]{:S(2)}) %all-to-all-start.7) | async-done | bytes 1048608 | tf_op jit(solution)/shard_map/all_to_all | solution.py:104
  83.0 1.6 fusion.14
  85.2 4.0 %all-to-all-start.9 = ((bf16[32,1,8]{2,1,0:T(2,128)(2,1)}), bf16[32,1,8]{2,1,0:T(2,128)(2,1)S(1)}, u32[]{:S(2)}, u32[]{:S(2)}) async-start(bf16[32,1,8]{2,1,0:T(2,128)(2,1)} %convert_element_type.401), calls=%async_computation.9 | async-start | bytes 32768 | tf_op jit(solution)/shard_map/all_to_all | solution.py:107
  91.4 4.7 %all-to-all-done.9 = bf16[32,1,8]{2,1,0:T(2,128)(2,1)S(1)} async-done(((bf16[32,1,8]{2,1,0:T(2,128)(2,1)}), bf16[32,1,8]{2,1,0:T(2,128)(2,1)S(1)}, u32[]{:S(2)}, u32[]{:S(2)}) %all-to-all-start.9) | async-done | bytes 544 | tf_op jit(solution)/shard_map/all_to_all | solution.py:107
  99.8 4.1 %all-to-all-start.6 = ((bf16[32,1,8]{2,1,0:T(2,128)(2,1)}), bf16[32,1,8]{2,1,0:T(2,128)(2,1)S(1)}, u32[]{:S(2)}, u32[]{:S(2)}) async-start(bf16[32,1,8]{2,1,0:T(2,128)(2,1)} %copy.246), calls=%async_computation.6 | async-start | bytes 32768 | tf_op jit(solution)/shard_map/all_to_all | solution.py:104
  104.0 2.3 slice_bitcast_fusion.1
  106.3 4.6 %all-to-all-done.6 = bf16[32,1,8]{2,1,0:T(2,128)(2,1)S(1)} async-done(((bf16[32,1,8]{2,1,0:T(2,128)(2,1)}), bf16[32,1,8]{2,1,0:T(2,128)(2,1)S(1)}, u32[]{:S(2)}, u32[]{:S(2)}) %all-to-all-start.6) | async-done | bytes 544 | tf_op jit(solution)/shard_map/all_to_all | solution.py:104
  111.6 4.2 %all-to-all-start.2 = ((bf16[32,8,2048]{2,1,0:T(8,128)(2,1)}), bf16[32,8,2048]{2,1,0:T(8,128)(2,1)S(1)}, u32[]{:S(2)}, u32[]{:S(2)}) async-start(bf16[32,8,2048]{2,1,0:T(8,128)(2,1)} %slice_bitcast_fusion.1), calls=%async_computation.2 | async-start | bytes 2097152 | tf_op jit(solution)/shard_map/all_to_all | solution.py:107
  116.4 71.3 %psum.7 = f32[2]{0:T(128)} all-reduce(f32[2]{0:T(128)} %convert_element_type.390), channel_id=1, replica_groups=mesh['section'=16,'expert'=32] {'expert'}, use_global_device_ids=true, to_apply=%region_33.37 | all-reduce | flops 2 | bytes 16 | tf_op jit(solution)/shard_map/psum | solution.py:150
  194.1 1.5 convert_reduce_fusion.4
  198.2 1.5 fusion.3
  199.7 4.6 %all-to-all-start.8 = ((bf16[32,8,2048]{2,1,0:T(8,128)(2,1)}), bf16[32,8,2048]{2,1,0:T(8,128)(2,1)}, u32[]{:S(2)}, u32[]{:S(2)}) async-start(bf16[32,8,2048]{2,1,0:T(8,128)(2,1)} %fusion.3), calls=%async_computation.8 | async-start | bytes 2097152 | tf_op jit(solution)/shard_map/all_to_all | solution.py:107
  208.1 1.7 fusion.47
  209.8 11.4 %all-to-all-done.8 = bf16[32,8,2048]{2,1,0:T(8,128)(2,1)} async-done(((bf16[32,8,2048]{2,1,0:T(8,128)(2,1)}), bf16[32,8,2048]{2,1,0:T(8,128)(2,1)}, u32[]{:S(2)}, u32[]{:S(2)}) %all-to-all-start.8) | async-done | bytes 1048608 | tf_op jit(solution)/shard_map/all_to_all | solution.py:107
  223.8 1.7 fusion.45
  228.0 3.9 %all-to-all-start.4 = ((bf16[32,8,2048]{2,1,0:T(8,128)(2,1)}), bf16[32,8,2048]{2,1,0:T(8,128)(2,1)S(1)}, u32[]{:S(2)}, u32[]{:S(2)}) async-start(bf16[32,8,2048]{2,1,0:T(8,128)(2,1)} %bitcast.34), calls=%async_computation.4 | async-start | bytes 2097152 | tf_op jit(solution)/shard_map/all_to_all | solution.py:104
  232.7 1.6 collective-permute-start
  235.3 1.9 collective-permute-done
  238.4 10.5 %all-to-all-done.4 = bf16[32,8,2048]{2,1,0:T(8,128)(2,1)S(1)} async-done(((bf16[32,8,2048]{2,1,0:T(8,128)(2,1)}), bf16[32,8,2048]{2,1,0:T(8,128)(2,1)S(1)}, u32[]{:S(2)}, u32[]{:S(2)}) %all-to-all-start.4) | async-done | bytes 1048608 | tf_op jit(solution)/shard_map/all_to_all | solution.py:104
  250.1 4.4 %all-to-all-start.3 = ((bf16[32,8,2048]{2,1,0:T(8,128)(2,1)}), bf16[32,8,2048]{2,1,0:T(8,128)(2,1)}, u32[]{:S(2)}, u32[]{:S(2)}) async-start(bf16[32,8,2048]{2,1,0:T(8,128)(2,1)} %bitcast.28), calls=%async_computation.3 | async-start | bytes 2097152 | tf_op jit(solution)/shard_map/all_to_all | solution.py:104
  261.7 9.8 %all-to-all-done.3 = bf16[32,8,2048]{2,1,0:T(8,128)(2,1)} async-done(((bf16[32,8,2048]{2,1,0:T(8,128)(2,1)}), bf16[32,8,2048]{2,1,0:T(8,128)(2,1)}, u32[]{:S(2)}, u32[]{:S(2)}) %all-to-all-start.3) | async-done | bytes 1048608 | tf_op jit(solution)/shard_map/all_to_all | solution.py:104
  272.6 3.9 %all-to-all-start.11 = ((bf16[32,8,2048]{2,1,0:T(8,128)(2,1)}), bf16[32,8,2048]{2,1,0:T(8,128)(2,1)S(1)}, u32[]{:S(2)}, u32[]{:S(2)}) async-start(bf16[32,8,2048]{2,1,0:T(8,128)(2,1)} %bitcast.67), calls=%async_computation.11 | async-start | bytes 2097152 | tf_op jit(solution)/shard_map/all_to_all | solution.py:104
  279.1 2.4 fusion.18
  281.5 2.9 divide_multiply_fusion
  285.3 2.1 convolution_convert_fusion
  287.4 6.1 %all-to-all-done.11 = bf16[32,8,2048]{2,1,0:T(8,128)(2,1)S(1)} async-done(((bf16[32,8,2048]{2,1,0:T(8,128)(2,1)}), bf16[32,8,2048]{2,1,0:T(8,128)(2,1)S(1)}, u32[]{:S(2)}, u32[]{:S(2)}) %all-to-all-start.11) | async-done | bytes 1048608 | tf_op jit(solution)/shard_map/all_to_all | solution.py:104
  293.5 1.6 fusion.17
  295.8 4.0 %all-to-all-start.13 = ((bf16[32,1,8]{2,1,0:T(2,128)(2,1)}), bf16[32,1,8]{2,1,0:T(2,128)(2,1)S(1)}, u32[]{:S(2)}, u32[]{:S(2)}) async-start(bf16[32,1,8]{2,1,0:T(2,128)(2,1)} %convert_element_type.402), calls=%async_computation.13 | async-start | bytes 32768 | tf_op jit(solution)/shard_map/all_to_all | solution.py:107
  300.9 5.8 %all-to-all-done.13 = bf16[32,1,8]{2,1,0:T(2,128)(2,1)S(1)} async-done(((bf16[32,1,8]{2,1,0:T(2,128)(2,1)}), bf16[32,1,8]{2,1,0:T(2,128)(2,1)S(1)}, u32[]{:S(2)}, u32[]{:S(2)}) %all-to-all-start.13) | async-done | bytes 544 | tf_op jit(solution)/shard_map/all_to_all | solution.py:107
  310.5 4.4 %all-to-all-start.10 = ((bf16[32,1,8]{2,1,0:T(2,128)(2,1)}), bf16[32,1,8]{2,1,0:T(2,128)(2,1)S(1)}, u32[]{:S(2)}, u32[]{:S(2)}) async-start(bf16[32,1,8]{2,1,0:T(2,128)(2,1)} %copy.257), calls=%async_computation.10 | async-start | bytes 32768 | tf_op jit(solution)/shard_map/all_to_all | solution.py:104
  314.9 2.3 slice_bitcast_fusion
  317.2 4.7 %all-to-all-done.10 = bf16[32,1,8]{2,1,0:T(2,128)(2,1)S(1)} async-done(((bf16[32,1,8]{2,1,0:T(2,128)(2,1)}), bf16[32,1,8]{2,1,0:T(2,128)(2,1)S(1)}, u32[]{:S(2)}, u32[]{:S(2)}) %all-to-all-start.10) | async-done | bytes 544 | tf_op jit(solution)/shard_map/all_to_all | solution.py:104
  322.5 4.2 %all-to-all-start.5 = ((bf16[32,8,2048]{2,1,0:T(8,128)(2,1)}), bf16[32,8,2048]{2,1,0:T(8,128)(2,1)S(1)}, u32[]{:S(2)}, u32[]{:S(2)}) async-start(bf16[32,8,2048]{2,1,0:T(8,128)(2,1)} %slice_bitcast_fusion), calls=%async_computation.5 | async-start | bytes 2097152 | tf_op jit(solution)/shard_map/all_to_all | solution.py:107
  326.8 1.6 fusion.77
  334.8 8.9 %all-to-all-done.5 = bf16[32,8,2048]{2,1,0:T(8,128)(2,1)S(1)} async-done(((bf16[32,8,2048]{2,1,0:T(8,128)(2,1)}), bf16[32,8,2048]{2,1,0:T(8,128)(2,1)S(1)}, u32[]{:S(2)}, u32[]{:S(2)}) %all-to-all-start.5) | async-done | bytes 1048608 | tf_op jit(solution)/shard_map/all_to_all | solution.py:107
  343.8 4.4 %all-to-all-start.12 = ((bf16[32,8,2048]{2,1,0:T(8,128)(2,1)}), bf16[32,8,2048]{2,1,0:T(8,128)(2,1)}, u32[]{:S(2)}, u32[]{:S(2)}) async-start(bf16[32,8,2048]{2,1,0:T(8,128)(2,1)} %fusion.2), calls=%async_computation.12 | async-start | bytes 2097152 | tf_op jit(solution)/shard_map/all_to_all | solution.py:107
  349.5 1.7 fusion.46
  352.0 13.2 %all-to-all-done.12 = bf16[32,8,2048]{2,1,0:T(8,128)(2,1)} async-done(((bf16[32,8,2048]{2,1,0:T(8,128)(2,1)}), bf16[32,8,2048]{2,1,0:T(8,128)(2,1)}, u32[]{:S(2)}, u32[]{:S(2)}) %all-to-all-start.12) | async-done | bytes 1048608 | tf_op jit(solution)/shard_map/all_to_all | solution.py:107
  367.8 1.7 fusion.44
  (381 shorter events, 80.7 us)
Async XLA Ops:
  0.6 74.7 %copy-start = (bf16[1,256,2048]{2,1,0:T(8,128)(2,1)S(1)}, bf16[1,256,2048]{2,1,0:T(8,128)(2,1)}, u32[]{:S(2)}) copy-start(bf16[1,256,2048]{2,1,0:T(8,128)(2,1)} %param.30) | copy-start | bytes 3145732
  8.4 14.3 %copy-start.54 = (s32[2,2,1,32,2]{3,4,2,1,0:T(2,128)S(1)}, s32[2,2,1,32,2]{3,4,2,1,0:T(2,128)}, u32[]{:S(2)}) copy-start(s32[2,2,1,32,2]{3,4,2,1,0:T(2,128)} %param.24) | copy-start | bytes 3076
  8.4 16.0 %copy-start.19 = (bf16[1,32,2048]{2,1,0:T(8,128)(2,1)S(1)}, bf16[1,32,2048]{2,1,0:T(8,128)(2,1)}, u32[]{:S(2)}) copy-start(bf16[1,32,2048]{2,1,0:T(8,128)(2,1)} %param.22) | copy-start | bytes 393220
  9.6 15.0 %copy-start.11 = (bf16[1,32,2048]{2,1,0:T(8,128)(2,1)S(1)}, bf16[1,32,2048]{2,1,0:T(8,128)(2,1)}, u32[]{:S(2)}) copy-start(bf16[1,32,2048]{2,1,0:T(8,128)(2,1)} %param.19) | copy-start | bytes 393220
  9.6 15.1 %copy-start.29 = (f32[1,2048]{1,0:T(1,128)S(1)}, f32[1,2048]{1,0:T(1,128)}, u32[]{:S(2)}) copy-start(f32[1,2048]{1,0:T(1,128)} %param.26) | copy-start | bytes 24580
  10.8 27.5 %all-to-all-start.1 = ((bf16[32,8,2048]{2,1,0:T(8,128)(2,1)}), bf16[32,8,2048]{2,1,0:T(8,128)(2,1)S(1)}, u32[]{:S(2)}, u32[]{:S(2)}) async-start(bf16[32,8,2048]{2,1,0:T(8,128)(2,1)} %bitcast.14), calls=%async_computation.1 | async-start | bytes 2097152 | tf_op jit(solution)/shard_map/all_to_all | solution.py:104
  23.3 22.1 %copy-start.58 = (s32[32,2]{0,1:T(2,128)}, s32[32,2]{0,1:T(2,128)S(1)}, u32[]{:S(2)}) copy-start(s32[32,2]{0,1:T(2,128)S(1)} %get-tuple-element.28) | copy-start | bytes 772
  24.6 23.0 %copy-start.9 = (bf16[2,1,32,2048]{3,2,1,0:T(8,128)(2,1)S(1)}, bf16[2,1,32,2048]{3,2,1,0:T(8,128)(2,1)}, u32[]{:S(2)}) copy-start(bf16[2,1,32,2048]{3,2,1,0:T(8,128)(2,1)} %param.21) | copy-start | bytes 786436
  24.8 14.7 %copy-start.98 = (f32[32]{0:T(128)}, f32[32]{0:T(128)S(1)}, u32[]{:S(2)}) copy-start(f32[32]{0:T(128)S(1)} %add_rsqrt_fusion.1) | copy-start | bytes 388
  39.5 21.4 %all-to-all-start = ((bf16[32,8,2048]{2,1,0:T(8,128)(2,1)}), bf16[32,8,2048]{2,1,0:T(8,128)(2,1)}, u32[]{:S(2)}, u32[]{:S(2)}) async-start(bf16[32,8,2048]{2,1,0:T(8,128)(2,1)} %bitcast.8), calls=%async_computation | async-start | bytes 2097152 | tf_op jit(solution)/shard_map/all_to_all | solution.py:104
  44.0 25.9 %copy-start.5 = (bf16[1,2048,256]{2,1,0:T(8,128)(2,1)S(1)}, bf16[1,2048,256]{2,1,0:T(8,128)(2,1)}, u32[]{:S(2)}) copy-start(bf16[1,2048,256]{2,1,0:T(8,128)(2,1)} %param.29) | copy-start | bytes 3145732
  62.1 20.9 %all-to-all-start.7 = ((bf16[32,8,2048]{2,1,0:T(8,128)(2,1)}), bf16[32,8,2048]{2,1,0:T(8,128)(2,1)S(1)}, u32[]{:S(2)}, u32[]{:S(2)}) async-start(bf16[32,8,2048]{2,1,0:T(8,128)(2,1)} %bitcast.50), calls=%async_computation.7 | async-start | bytes 2097152 | tf_op jit(solution)/shard_map/all_to_all | solution.py:104
  77.4 11.8 %copy-start.53 = (s32[32,2,1]{1,0,2:T(8,128)S(1)}, s32[32,2,1]{1,0,2:T(8,128)}, u32[]{:S(2)}) copy-start(s32[32,2,1]{1,0,2:T(8,128)} %copy.243) | copy-start | bytes 772
  85.2 10.8 %all-to-all-start.9 = ((bf16[32,1,8]{2,1,0:T(2,128)(2,1)}), bf16[32,1,8]{2,1,0:T(2,128)(2,1)S(1)}, u32[]{:S(2)}, u32[]{:S(2)}) async-start(bf16[32,1,8]{2,1,0:T(2,128)(2,1)} %convert_element_type.401), calls=%async_computation.9 | async-start | bytes 32768 | tf_op jit(solution)/shard_map/all_to_all | solution.py:107
  99.8 11.1 %all-to-all-start.6 = ((bf16[32,1,8]{2,1,0:T(2,128)(2,1)}), bf16[32,1,8]{2,1,0:T(2,128)(2,1)S(1)}, u32[]{:S(2)}, u32[]{:S(2)}) async-start(bf16[32,1,8]{2,1,0:T(2,128)(2,1)} %copy.246), calls=%async_computation.6 | async-start | bytes 32768 | tf_op jit(solution)/shard_map/all_to_all | solution.py:104
  104.0 11.8 %copy-start.66 = (s32[32]{0:T(128)S(1)}, s32[32]{0:T(128)}, u32[]{:S(2)}) copy-start(s32[32]{0:T(128)} %get-tuple-element.60) | copy-start | bytes 388
  104.0 85.1 %copy-start.72 = (s32[1,1,1,32,2]{3,4,2,1,0:T(2,128)S(1)}, s32[1,1,1,32,2]{3,4,2,1,0:T(2,128)}, u32[]{:S(2)}) copy-start(s32[1,1,1,32,2]{3,4,2,1,0:T(2,128)} %get-tuple-element.42) | copy-start | bytes 772
  104.0 90.1 %copy-start.62 = (s32[32,2]{0,1:T(2,128)S(1)}, s32[32,2]{0,1:T(2,128)}, u32[]{:S(2)}) copy-start(s32[32,2]{0,1:T(2,128)} %get-tuple-element.56) | copy-start | bytes 772
  111.6 88.2 %all-to-all-start.2 = ((bf16[32,8,2048]{2,1,0:T(8,128)(2,1)}), bf16[32,8,2048]{2,1,0:T(8,128)(2,1)S(1)}, u32[]{:S(2)}, u32[]{:S(2)}) async-start(bf16[32,8,2048]{2,1,0:T(8,128)(2,1)} %slice_bitcast_fusion.1), calls=%async_computation.2 | async-start | bytes 2097152 | tf_op jit(solution)/shard_map/all_to_all | solution.py:107
  199.7 21.5 %all-to-all-start.8 = ((bf16[32,8,2048]{2,1,0:T(8,128)(2,1)}), bf16[32,8,2048]{2,1,0:T(8,128)(2,1)}, u32[]{:S(2)}, u32[]{:S(2)}) async-start(bf16[32,8,2048]{2,1,0:T(8,128)(2,1)} %fusion.3), calls=%async_computation.8 | async-start | bytes 2097152 | tf_op jit(solution)/shard_map/all_to_all | solution.py:107
  209.8 22.1 %copy-start.10 = (f32[32,2048]{1,0:T(8,128)}, f32[32,2048]{1,0:T(8,128)S(1)}, u32[]{:S(2)}) copy-start(f32[32,2048]{1,0:T(8,128)S(1)} %fusion.47) | copy-start | bytes 786436
  226.6 50.0 %copy-start.92 = (f32[32]{0:T(128)}, f32[32]{0:T(128)S(1)}, u32[]{:S(2)}) copy-start(f32[32]{0:T(128)S(1)} %fusion.165) | copy-start | bytes 388
  226.9 10.3 %copy-start.34 = (bf16[1,32,2048]{2,1,0:T(8,128)(2,1)S(1)}, bf16[1,32,2048]{2,1,0:T(8,128)(2,1)}, u32[]{:S(2)}) copy-start(bf16[1,32,2048]{2,1,0:T(8,128)(2,1)} %param.20) | copy-start | bytes 393220
  228.0 20.9 %all-to-all-start.4 = ((bf16[32,8,2048]{2,1,0:T(8,128)(2,1)}), bf16[32,8,2048]{2,1,0:T(8,128)(2,1)S(1)}, u32[]{:S(2)}, u32[]{:S(2)}) async-start(bf16[32,8,2048]{2,1,0:T(8,128)(2,1)} %bitcast.34), calls=%async_computation.4 | async-start | bytes 2097152 | tf_op jit(solution)/shard_map/all_to_all | solution.py:104
  232.7 4.5 %collective-permute-start = (bf16[32,2048]{1,0:T(8,128)(2,1)}, bf16[32,2048]{1,0:T(8,128)(2,1)S(1)}, u32[]{:S(2)}, u32[]{:S(2)}) collective-permute-start(bf16[32,2048]{1,0:T(8,128)(2,1)} %fusion.74), channel_id=1, source_target_pairs={{0,32},{32,64},{64,96},{96,128},{128,160},{160,192},{192,224},{224... | collective-permute-start | bytes 393224 | tf_op jit(solution)/shard_map/ppermute | solution.py:21
  235.2 19.3 %copy-start.95 = (f32[32]{0:T(128)S(1)}, f32[32]{0:T(128)}, u32[]{:S(2)}) copy-start(f32[32]{0:T(128)} %copy-done.94) | copy-start | bytes 388
  235.3 19.3 %copy-start.20 = (bf16[1,32,2048]{2,1,0:T(8,128)(2,1)S(1)}, bf16[1,32,2048]{2,1,0:T(8,128)(2,1)}, u32[]{:S(2)}) copy-start(bf16[1,32,2048]{2,1,0:T(8,128)(2,1)} %param.22) | copy-start | bytes 393220
  235.3 19.3 %copy-start.84 = (f32[32]{0:T(128)S(1)}, f32[32]{0:T(128)}, u32[]{:S(2)}) copy-start(f32[32]{0:T(128)} %copy-done.83) | copy-start | bytes 388
  238.3 19.8 %copy-start.79 = (s32[32,2,1]{0,1,2:T(2,128)S(1)}, s32[32,2,1]{0,1,2:T(2,128)}, u32[]{:S(2)}) copy-start(s32[32,2,1]{0,1,2:T(2,128)} %get-tuple-element.48) | copy-start | bytes 772
  238.3 20.0 %copy-start.73 = (f32[32,2]{0,1:T(2,128)S(1)}, f32[32,2]{0,1:T(2,128)}, u32[]{:S(2)}) copy-start(f32[32,2]{0,1:T(2,128)} %get-tuple-element.63) | copy-start | bytes 772
  238.3 20.7 %copy-start.78 = (s32[32,2,1]{0,1,2:T(2,128)S(1)}, s32[32,2,1]{0,1,2:T(2,128)}, u32[]{:S(2)}) copy-start(s32[32,2,1]{0,1,2:T(2,128)} %get-tuple-element.51) | copy-start | bytes 772
  238.3 20.9 %copy-start.87 = (pred[32,2]{0,1:T(4,128)(4,1)S(1)}, pred[32,2]{0,1:T(4,128)(4,1)}, u32[]{:S(2)}) copy-start(pred[32,2]{0,1:T(4,128)(4,1)} %get-tuple-element.27) | copy-start | bytes 196
  238.4 21.6 %copy-start.77 = (s32[32,2]{0,1:T(2,128)S(1)}, s32[32,2]{0,1:T(2,128)}, u32[]{:S(2)}) copy-start(s32[32,2]{0,1:T(2,128)} %get-tuple-element.55) | copy-start | bytes 772
  238.4 23.1 %copy-start.21 = (bf16[1,32,2048]{2,1,0:T(8,128)(2,1)S(1)}, bf16[1,32,2048]{2,1,0:T(8,128)(2,1)}, u32[]{:S(2)}) copy-start(bf16[1,32,2048]{2,1,0:T(8,128)(2,1)} %param.23) | copy-start | bytes 393220
  250.1 21.4 %all-to-all-start.3 = ((bf16[32,8,2048]{2,1,0:T(8,128)(2,1)}), bf16[32,8,2048]{2,1,0:T(8,128)(2,1)}, u32[]{:S(2)}, u32[]{:S(2)}) async-start(bf16[32,8,2048]{2,1,0:T(8,128)(2,1)} %bitcast.28), calls=%async_computation.3 | async-start | bytes 2097152 | tf_op jit(solution)/shard_map/all_to_all | solution.py:104
  254.7 6.7 %collective-permute-start.1 = (bf16[32,2048]{1,0:T(8,128)(2,1)S(1)}, bf16[32,2048]{1,0:T(8,128)(2,1)S(1)}, u32[]{:S(2)}, u32[]{:S(2)}) collective-permute-start(bf16[32,2048]{1,0:T(8,128)(2,1)S(1)} %fusion.83), channel_id=1, source_target_pairs={{32,0},{64,32},{96,64},{128,96},{160,128},{192,160},{224,192},{256... | collective-permute-start | bytes 393224 | tf_op jit(solution)/shard_map/ppermute | solution.py:21
  261.5 11.2 %copy-start.25 = (bf16[32,2048]{1,0:T(8,128)(2,1)}, bf16[32,2048]{1,0:T(8,128)(2,1)S(1)}, u32[]{:S(2)}) copy-start(bf16[32,2048]{1,0:T(8,128)(2,1)S(1)} %collective-permute-done.1) | copy-start | bytes 393220
  272.6 20.9 %all-to-all-start.11 = ((bf16[32,8,2048]{2,1,0:T(8,128)(2,1)}), bf16[32,8,2048]{2,1,0:T(8,128)(2,1)S(1)}, u32[]{:S(2)}, u32[]{:S(2)}) async-start(bf16[32,8,2048]{2,1,0:T(8,128)(2,1)} %bitcast.67), calls=%async_computation.11 | async-start | bytes 2097152 | tf_op jit(solution)/shard_map/all_to_all | solution.py:104
  287.4 12.4 %copy-start.13 = (bf16[32,2048]{1,0:T(8,128)(2,1)S(1)}, bf16[32,2048]{1,0:T(8,128)(2,1)}, u32[]{:S(2)}) copy-start(bf16[32,2048]{1,0:T(8,128)(2,1)} %copy-done.12) | copy-start | bytes 393220
  287.4 12.4 %copy-start.31 = (f32[1,2048]{1,0:T(1,128)S(1)}, f32[1,2048]{1,0:T(1,128)}, u32[]{:S(2)}) copy-start(f32[1,2048]{1,0:T(1,128)} %param.26) | copy-start | bytes 24580
  287.4 12.4 %copy-start.36 = (bf16[1,2048,8]{1,2,0:T(8,128)(2,1)S(1)}, bf16[1,2048,8]{1,2,0:T(8,128)(2,1)}, u32[]{:S(2)}) copy-start(bf16[1,2048,8]{1,2,0:T(8,128)(2,1)} %param.27) | copy-start | bytes 98308
  287.4 12.4 %copy-start.97 = (f32[32]{0:T(128)S(1)}, f32[32]{0:T(128)}, u32[]{:S(2)}) copy-start(f32[32]{0:T(128)} %copy-done.96) | copy-start | bytes 388
  295.8 10.9 %all-to-all-start.13 = ((bf16[32,1,8]{2,1,0:T(2,128)(2,1)}), bf16[32,1,8]{2,1,0:T(2,128)(2,1)S(1)}, u32[]{:S(2)}, u32[]{:S(2)}) async-start(bf16[32,1,8]{2,1,0:T(2,128)(2,1)} %convert_element_type.402), calls=%async_computation.13 | async-start | bytes 32768 | tf_op jit(solution)/shard_map/all_to_all | solution.py:107
  310.5 11.4 %all-to-all-start.10 = ((bf16[32,1,8]{2,1,0:T(2,128)(2,1)}), bf16[32,1,8]{2,1,0:T(2,128)(2,1)S(1)}, u32[]{:S(2)}, u32[]{:S(2)}) async-start(bf16[32,1,8]{2,1,0:T(2,128)(2,1)} %copy.257), calls=%async_computation.10 | async-start | bytes 32768 | tf_op jit(solution)/shard_map/all_to_all | solution.py:104
  314.9 15.0 %copy-start.74 = (s32[32,2]{0,1:T(2,128)S(1)}, s32[32,2]{0,1:T(2,128)}, u32[]{:S(2)}) copy-start(s32[32,2]{0,1:T(2,128)} %get-tuple-element.39) | copy-start | bytes 772
  322.5 21.2 %all-to-all-start.5 = ((bf16[32,8,2048]{2,1,0:T(8,128)(2,1)}), bf16[32,8,2048]{2,1,0:T(8,128)(2,1)S(1)}, u32[]{:S(2)}, u32[]{:S(2)}) async-start(bf16[32,8,2048]{2,1,0:T(8,128)(2,1)} %slice_bitcast_fusion), calls=%async_computation.5 | async-start | bytes 2097152 | tf_op jit(solution)/shard_map/all_to_all | solution.py:107
  334.8 13.6 %copy-start.46 = (s32[1024]{0:T(1024)S(1)}, s32[1024]{0:T(1024)}, u32[]{:S(2)}) copy-start(s32[1024]{0:T(1024)} %pad_clamp_fusion.2) | copy-start | bytes 12292
  343.8 21.4 %all-to-all-start.12 = ((bf16[32,8,2048]{2,1,0:T(8,128)(2,1)}), bf16[32,8,2048]{2,1,0:T(8,128)(2,1)}, u32[]{:S(2)}, u32[]{:S(2)}) async-start(bf16[32,8,2048]{2,1,0:T(8,128)(2,1)} %fusion.2), calls=%async_computation.12 | async-start | bytes 2097152 | tf_op jit(solution)/shard_map/all_to_all | solution.py:107
  (71 other events, 214.3 us)
where the time goes:
time: 374 us; the launch traced here: 372 us
  waiting for transfers between devices  113 us (30%)
  blocking collectives  71.3 us (19%)
  starting transfers between devices  68 us (18%)
  local copies, waits for them, and re-layouts  49.2 us (13%)
  other arithmetic  39.3 us (11%)
  matrix products  25.7 us (7%)
  between operations  5.49 us (1%)
    psum x1, blocking collectives, on_device(): lax.psum(jnp.sum(counts[0, :, 0], axis=-1).astype(jnp.float32), 'expert')  71.3 us
    all_to_all x8, waiting for transfers between devices, route_rows(): lax.all_to_all(shortened(outgoing), 'expert', split_axis=0, concat_axis=0...  66.3 us
    all_to_all x6, waiting for transfers between devices, route_rows(): lax.all_to_all(shortened(work(*received)), 'expert', split_axis=0, concat...  44 us
    all_to_all x8, starting transfers between devices, route_rows(): lax.all_to_all(shortened(outgoing), 'expert', split_axis=0, concat_axis=0...  39.7 us
    all_to_all x6, starting transfers between devices, route_rows(): lax.all_to_all(shortened(work(*received)), 'expert', split_axis=0, concat...  25.5 us
  transfers between devices with their start and end apart: 16, of which 15 were waited for; matrix products, arithmetic and copies ran while one was open for 19% of the time, Pallas kernels for 0%

commit v1 on v0

v1 whole, which is shorter than its diff:
```python
import jax
import jax.numpy as jnp
from jax import lax
from jax.sharding import PartitionSpec as P

SPLIT = 4
TICKS = 2
LANES = 128


def from_behind(block, axis, distance):
    devices = range(lax.axis_size(axis))
    route = [(i - distance, i) for i in devices if i - distance in devices]
    return lax.ppermute(block, axis, route)


def expert_work(rows, carried, gate_q, up_q, down_q, capacity):
    sources, pair_rows, width = rows.shape
    hidden_q = gate_q.shape[1]
    flat = rows.reshape(sources * pair_rows, width)
    pre_gate = jnp.dot(flat, gate_q, preferred_element_type=jnp.float32)
    pre_up = jnp.dot(flat, up_q, preferred_element_type=jnp.float32)
    sigmoid_g = jax.nn.sigmoid(pre_gate)
    activated = pre_gate * sigmoid_g
    hidden = (activated * pre_up).astype(jnp.bfloat16)

    def half(value, which):
        paired = value.reshape(sources, 2, capacity, hidden_q)
        return paired[:, which].reshape(sources * capacity, hidden_q)

    y_part = jnp.dot(half(hidden, 0), down_q, preferred_element_type=jnp.float32)
    grads = carried[:, :, :width].reshape(sources * capacity, width)
    scales = carried[:, :, width].reshape(sources * capacity, 1).astype(jnp.float32)
    plain_h = jnp.dot(grads, down_q.T, preferred_element_type=jnp.float32)
    inner_dot = jnp.sum(plain_h * half(hidden, 1).astype(jnp.float32), axis=-1, keepdims=True)
    back_h = plain_h * scales
    slope_g = half(sigmoid_g, 1)
    d_gate = back_h * half(pre_up, 1) * slope_g * (1.0 + half(pre_gate, 1) * (1.0 - slope_g))
    d_up = back_h * half(activated, 1)
    dn_part = jnp.dot(
        d_gate.astype(jnp.bfloat16), gate_q.T, preferred_element_type=jnp.float32
    ) + jnp.dot(d_up.astype(jnp.bfloat16), up_q.T, preferred_element_type=jnp.float32)
    dots = jnp.broadcast_to(inner_dot, (sources * capacity, LANES))
    joined = jnp.concatenate([y_part, dn_part, dots], axis=-1).astype(jnp.bfloat16)
    return joined.reshape(sources, capacity, 2 * width + LANES)


def spread(block, experts):
    repeated = jnp.broadcast_to(block[:, None], (experts, SPLIT) + block.shape[1:])
    return repeated.reshape((experts * SPLIT,) + block.shape[1:])


def on_device(
    section_in,
    new_batch,
    stashed,
    grad_in,
    loss_grad,
    routes,
    counts,
    norm_gain,
    w_router,
    w_gate,
    w_up,
    w_down,
    lam,
):
    f32, bf16 = jnp.float32, jnp.bfloat16
    section_pos = lax.axis_index("section")
    last_section = lax.axis_size("section") - 1
    tok_rows, width = section_in.shape[1:]
    top_slots = routes.shape[-1]
    experts = w_router.shape[-1]
    capacity = SPLIT * min(
        tok_rows // (2 * SPLIT), 5 * tok_rows * top_slots // (4 * experts * SPLIT)
    )
    slots = experts * capacity
    entries = tok_rows * top_slots
    share_total = tok_rows * lax.axis_size("expert") * top_slots
    gain_row = norm_gain[0]
    router = w_router[0]
    router_t = router.astype(f32).T
    gate_cols, up_cols, down_rows = w_gate[0], w_up[0], w_down[0]
    route = routes[:, :, 0]
    count = counts[:, :, 0]
    flat = route.reshape(2, TICKS, entries)
    earlier = jnp.arange(entries)[None, :] < jnp.arange(entries)[:, None]
    rank = jnp.sum(
        ((flat[..., :, None] == flat[..., None, :]) & earlier).astype(jnp.int32), axis=-1
    )
    target = (flat * capacity + rank).reshape(2, TICKS, tok_rows, top_slots)
    live = jnp.arange(top_slots, dtype=jnp.int32) < count[..., None]
    table = ((target[..., None] == jnp.arange(slots)) & live[..., None]).astype(f32)
    chosen = (route[..., None] == jnp.arange(experts)).astype(f32)
    dispatch = jnp.sum(table, axis=3).astype(bf16)
    live = live.astype(f32)
    own_totals = jnp.sum(count[0], axis=-1).astype(f32)

    def norm_of(values):
        values = values.astype(f32)
        inverse = lax.rsqrt(jnp.mean(values * values, axis=-1, keepdims=True) + 1e-05)
        return values * inverse, inverse

    def picked_of(normed, m, k):
        logits = jnp.dot(normed, router, preferred_element_type=f32)
        return jnp.sum(chosen[m, k] * logits[:, None, :], axis=-1)

    def placed(m, k, rows):
        return lax.dot_general(
            dispatch[m, k], rows, (((0,), (0,)), ((), ())), preferred_element_type=f32
        ).astype(bf16)

    backs = []
    for k in range(TICKS):
        unit, inverse = norm_of(stashed[k, 0])
        normed = (unit * gain_row).astype(bf16)
        picked = picked_of(normed, 1, k)
        gate = jax.nn.softplus(picked) * live[1, k]
        scale = jnp.sum(table[1, k] * gate[:, :, None], axis=(0, 1))
        backs.append((unit, inverse, placed(1, k, normed), picked, scale))

    weight = lam[0]
    forward_x = section_in[0]
    cotangent = grad_in[0]
    fwd_list = []
    grad_list = []
    totals = None
    for k in range(TICKS):
        if k > 0:
            arriving = from_behind(fwd_list[-1], "section", 1)
            forward_x = jnp.where(section_pos == 0, new_batch[k - 1], arriving)
            coming = from_behind(grad_list[-1], "section", -1)
            cotangent = jnp.where(section_pos == last_section, loss_grad[k - 1], coming)
        unit_b, inverse_b, rows_b, picked_b, scale_b = backs[k]
        unit_f, _ = norm_of(forward_x)
        normed_f = (unit_f * gain_row).astype(bf16)
        gate_f = jax.nn.softplus(picked_of(normed_f, 0, k)) * live[0, k]
        rows = jnp.concatenate(
            [
                placed(0, k, normed_f).reshape(experts, capacity, width),
                rows_b.reshape(experts, capacity, width),
            ],
            axis=1,
        )
        lane = jnp.arange(LANES)
        extra = jnp.where(
            lane == 0,
            scale_b[:, None],
            jnp.where(lane == 1, own_totals[0], jnp.where(lane == 2, own_totals[1], 0.0)),
        ).astype(bf16)
        carried = jnp.concatenate([placed(1, k, cotangent), extra], axis=1)
        carried = carried.reshape(experts, capacity, width + LANES)
        got_rows = lax.all_to_all(spread(rows, experts), "expert", 0, 0, tiled=True)
        got_carried = lax.all_to_all(spread(carried, experts), "expert", 0, 0, tiled=True)
        if totals is None:
            seen = got_carried[:, 0, width + 1 : width + 1 + TICKS].astype(f32)
            totals = jnp.sum(seen, axis=0)
        partial = expert_work(got_rows, got_carried, gate_cols, up_cols, down_rows, capacity)
        back = lax.all_to_all(partial, "expert", 0, 0, tiled=True)
        summed = jnp.sum(
            back.astype(f32).reshape(experts, SPLIT, capacity, 2 * width + LANES), axis=1
        ).reshape(slots, 2 * width + LANES)
        combine_f = jnp.sum(table[0, k] * gate_f[:, :, None], axis=1)
        out_f = forward_x.astype(f32) + jnp.dot(
            combine_f, summed[:, :width], precision=lax.Precision.HIGHEST
        )
        dots = jnp.sum(table[1, k] * summed[:, 2 * width], axis=-1)
        dpick = (dots + weight) * jax.nn.sigmoid(picked_b) * live[1, k]
        dlogit = jnp.sum(chosen[1, k] * dpick[:, :, None], axis=1)
        dnorm = jnp.dot(
            jnp.sum(table[1, k], axis=1),
            summed[:, width : 2 * width],
            precision=lax.Precision.HIGHEST,
        ) + jnp.dot(dlogit, router_t, precision=lax.Precision.HIGHEST)
        scaled = dnorm * gain_row
        along = jnp.mean(scaled * unit_b, axis=-1, keepdims=True)
        grad_x = cotangent.astype(f32) + inverse_b * (scaled - unit_b * along)
        fwd_list.append(out_f.astype(bf16))
        grad_list.append(grad_x.astype(bf16))
        weight = weight * jnp.exp(4.0 * (totals[k] / share_total - 0.5))
    return (jnp.stack(fwd_list)[:, None], jnp.stack(grad_list)[:, None], weight.reshape(1))


def solution(mesh):
    in_specs = (
        P("section", "expert", None),
        P(None, "expert", None),
        P(None, "section", "expert", None),
        P("section", "expert", None),
        P(None, "expert", None),
        P(None, None, "section", "expert", None),
        P(None, None, "section", "expert"),
        P("section", None),
        P("section", None, None),
        P("section", None, "expert"),
        P("section", None, "expert"),
        P("section", "expert", None),
        P("section"),
    )
    out_specs = (
        P(None, "section", "expert", None),
        P(None, "section", "expert", None),
        P("section"),
    )
    return jax.shard_map(
        on_device, mesh=mesh, in_specs=in_specs, out_specs=out_specs, check_vma=False
    )
```

time: 374 us -> 281 us (0.75)
  blocking collectives: 71.3 us -> 0 us
  waiting for transfers between devices: 113 us -> 149 us
  starting transfers between devices: 68 us -> 38.3 us
  other arithmetic: 39.3 us -> 19.3 us
  local copies, waits for them, and re-layouts: 49.2 us -> 36.9 us
    psum x1 -> x0, blocking collectives: 71.3 us -> none  [on_device(): lax.psum(jnp.sum(counts[0, :, 0], axis=-1).astype(jnp.float32), 'expert')]
    all_to_all x14 -> x6, waiting for transfers between devices: 110 us -> 142 us  [the longest x2 54.9 us: on_device(): got_rows = lax.all_to_all(spread(rows, experts), 'expert', 0, 0, tiled=True)]
    all_to_all x14 -> x6, starting transfers between devices: 65.1 us -> 35.4 us  [the longest x2 16.7 us: on_device(): lax.all_to_all(spread(carried, experts), 'expert', 0, 0, tiled=True)]
    another operation x0 -> x19, local copies, waits for them, and re-layouts: none -> 20 us  [the longest x16 19.7 us: half(): return paired[:, which].reshape(sources * capacity, hidden_q)]
    gather x34 -> x0, local copies, waits for them, and re-layouts: 13.2 us -> none  [the longest x10 4.8 us: on_device(): jnp.take_along_axis(jnp.dot(normed_b, router, preferred_element_type=jnp....]
    reduce_sum x26 -> x18, other arithmetic: 19.4 us -> 8.25 us  [the longest x3 2.29 us: norm_of(): jnp.mean(values * values, axis=-1, keepdims=True) + 1e-05]
    reshape x6 -> x0, local copies, waits for them, and re-layouts: 5.01 us -> none  [the longest x2 4.65 us: work(): projected.reshape(leading + (width,))]
    ppermute x2, waiting for transfers between devices: 2.69 us -> 6.94 us  [from_behind(): return lax.ppermute(block, axis, route)]
  transfers between devices with their start and end apart: 16 -> 8, of which waited for: 15 -> 8; matrix products, arithmetic and copies ran while one was open for 19% -> 2% of each run, Pallas kernels for 0% -> 0%
where the time goes in v1:
time: 281 us; the launch traced here: 277 us
  waiting for transfers between devices  149 us (53%)
  starting transfers between devices  38.3 us (14%)
  local copies, waits for them, and re-layouts  36.9 us (13%)
  matrix products  28.6 us (10%)
  other arithmetic  19.3 us (7%)
  between operations  4.72 us (2%)
    all_to_all x2, waiting for transfers between devices, on_device(): got_rows = lax.all_to_all(spread(rows, experts), 'expert', 0, 0, tiled=True)  54.9 us
    all_to_all x2, waiting for transfers between devices, on_device(): back = lax.all_to_all(partial, 'expert', 0, 0, tiled=True)  53.2 us
    all_to_all x2, waiting for transfers between devices, on_device(): lax.all_to_all(spread(carried, experts), 'expert', 0, 0, tiled=True)  34.2 us
    another operation x16, local copies, waits for them, and re-layouts, half(): return paired[:, which].reshape(sources * capacity, hidden_q)  19.7 us
    all_to_all x2, starting transfers between devices, on_device(): lax.all_to_all(spread(carried, experts), 'expert', 0, 0, tiled=True)  16.7 us
    all_to_all x2, starting transfers between devices, on_device(): got_rows = lax.all_to_all(spread(rows, experts), 'expert', 0, 0, tiled=True)  9.54 us
    all_to_all x2, starting transfers between devices, on_device(): back = lax.all_to_all(partial, 'expert', 0, 0, tiled=True)  9.12 us
    ppermute x2, waiting for transfers between devices, from_behind(): return lax.ppermute(block, axis, route)  6.94 us
  transfers between devices with their start and end apart: 8, of which 8 were waited for; matrix products, arithmetic and copies ran while one was open for 2% of the time, Pallas kernels for 0%

profile of v1, /device:TPU:1, one launch (start us, length us, event | category | flops | bytes accessed | tf_op | source)
XLA Modules:
  0.0 276.9 jit_solution(6713369083854749841)
XLA Ops:
  3.9 1.1 fusion.64
  6.7 1.1 fusion.105
  7.8 1.1 fusion.87
  9.1 1.3 compare_select_fusion.5
  11.1 1.1 convolution_convert_fusion.5
  13.5 10.5 %all-to-all-start.1 = ((bf16[32,8,2176]{2,1,0:T(8,128)(2,1)}), bf16[32,8,2176]{2,1,0:T(8,128)(2,1)S(1)}, u32[]{:S(2)}, u32[]{:S(2)}) async-start(bf16[32,8,2176]{2,1,0:T(8,128)(2,1)} %bitcast.30), calls=%async_computation.1 | async-start | bytes 2228224 | tf_op jit(solution)/shard_map/all_to_all | solution.py:154
  24.6 17.1 %all-to-all-done.1 = bf16[32,8,2176]{2,1,0:T(8,128)(2,1)S(1)} async-done(((bf16[32,8,2176]{2,1,0:T(8,128)(2,1)}), bf16[32,8,2176]{2,1,0:T(8,128)(2,1)S(1)}, u32[]{:S(2)}, u32[]{:S(2)}) %all-to-all-start.1) | async-done | bytes 1114144 | tf_op jit(solution)/shard_map/all_to_all | solution.py:154
  41.7 1.7 broadcast_in_dim.64
  43.4 4.7 %all-to-all-start = ((bf16[32,16,2048]{2,1,0:T(8,128)(2,1)}), bf16[32,16,2048]{2,1,0:T(8,128)(2,1)}, u32[]{:S(2)}, u32[]{:S(2)}) async-start(bf16[32,16,2048]{2,1,0:T(8,128)(2,1)} %bitcast.15), calls=%async_computation | async-start | bytes 4194304 | tf_op jit(solution)/shard_map/all_to_all | solution.py:153
  49.6 26.9 %all-to-all-done = bf16[32,16,2048]{2,1,0:T(8,128)(2,1)} async-done(((bf16[32,16,2048]{2,1,0:T(8,128)(2,1)}), bf16[32,16,2048]{2,1,0:T(8,128)(2,1)}, u32[]{:S(2)}, u32[]{:S(2)}) %all-to-all-start) | async-done | bytes 2097184 | tf_op jit(solution)/shard_map/all_to_all | solution.py:153
  76.4 2.3 fusion.23
  79.5 3.4 %fusion.127 = (f32[512,256]{1,0:T(8,128)S(1)}, bf16[512,256]{1,0:T(8,128)(2,1)}, f32[512,256]{1,0:T(8,128)}, f32[512,256]{1,0:T(8,128)}) fusion(f32[512,256]{1,0:T(8,128)S(1)} %fusion.23, bf16[512,2048]{1,0:T(8,128)(2,1)} %bitcast.16, bf16[1,2048,256]{2,1,0:T(8,128)(2,1)S(1)} %copy-done), kind=kOutput, calls=%fused_computation.230 | convolution fusion | flops 537657344 | bytes 5505024 | tf_op jit(solution)/shard_map/dot_general | solution.py:21
  83.6 1.8 copy.136
  85.4 1.7 slice_bitcast_fusion.11
  87.1 1.8 copy.129
  88.9 1.6 fusion.75
  90.5 1.8 copy.138
  92.3 2.5 convolution_convert_fusion.1
  94.7 1.2 multiply_reduce_fusion.1
  97.2 1.7 slice_bitcast_fusion.9
  98.9 1.1 copy.134
  102.1 1.5 pad_maximum_fusion
  103.7 4.6 %all-to-all-start.2 = ((bf16[32,8,4224]{2,1,0:T(8,128)(2,1)}), bf16[32,8,4224]{2,1,0:T(8,128)(2,1)S(1)}, u32[]{:S(2)}, u32[]{:S(2)}) async-start(bf16[32,8,4224]{2,1,0:T(8,128)(2,1)} %pad_maximum_fusion), calls=%async_computation.2 | async-start | bytes 4325376 | tf_op jit(solution)/shard_map/all_to_all | solution.py:159
  108.9 1.4 slice_reduce_fusion.2
  110.3 27.0 %all-to-all-done.2 = bf16[32,8,4224]{2,1,0:T(8,128)(2,1)S(1)} async-done(((bf16[32,8,4224]{2,1,0:T(8,128)(2,1)}), bf16[32,8,4224]{2,1,0:T(8,128)(2,1)S(1)}, u32[]{:S(2)}, u32[]{:S(2)}) %all-to-all-start.2) | async-done | bytes 2162720 | tf_op jit(solution)/shard_map/all_to_all | solution.py:159
  139.8 1.6 collective-permute-start
  141.4 1.9 collective-permute-done
  145.3 1.3 collective-permute-start.1
  146.7 5.0 %collective-permute-done.1 = bf16[32,2048]{1,0:T(8,128)(2,1)S(1)} collective-permute-done((bf16[32,2048]{1,0:T(8,128)(2,1)S(1)}, bf16[32,2048]{1,0:T(8,128)(2,1)S(1)}, u32[]{:S(2)}, u32[]{:S(2)}) %collective-permute-start.1) | collective-permute-done | bytes 131104 | tf_op jit(solution)/shard_map/ppermute | solution.py:14
  152.4 1.1 broadcast_in_dim.127
  153.5 6.2 %all-to-all-start.4 = ((bf16[32,8,2176]{2,1,0:T(8,128)(2,1)}), bf16[32,8,2176]{2,1,0:T(8,128)(2,1)S(1)}, u32[]{:S(2)}, u32[]{:S(2)}) async-start(bf16[32,8,2176]{2,1,0:T(8,128)(2,1)} %bitcast.65), calls=%async_computation.4 | async-start | bytes 2228224 | tf_op jit(solution)/shard_map/all_to_all | solution.py:154
  160.4 17.1 %all-to-all-done.4 = bf16[32,8,2176]{2,1,0:T(8,128)(2,1)S(1)} async-done(((bf16[32,8,2176]{2,1,0:T(8,128)(2,1)}), bf16[32,8,2176]{2,1,0:T(8,128)(2,1)S(1)}, u32[]{:S(2)}, u32[]{:S(2)}) %all-to-all-start.4) | async-done | bytes 1114144 | tf_op jit(solution)/shard_map/all_to_all | solution.py:154
  177.5 1.7 broadcast_in_dim.124
  179.2 4.9 %all-to-all-start.3 = ((bf16[32,16,2048]{2,1,0:T(8,128)(2,1)}), bf16[32,16,2048]{2,1,0:T(8,128)(2,1)}, u32[]{:S(2)}, u32[]{:S(2)}) async-start(bf16[32,16,2048]{2,1,0:T(8,128)(2,1)} %bitcast.55), calls=%async_computation.3 | async-start | bytes 4194304 | tf_op jit(solution)/shard_map/all_to_all | solution.py:153
  184.2 28.0 %all-to-all-done.3 = bf16[32,16,2048]{2,1,0:T(8,128)(2,1)} async-done(((bf16[32,16,2048]{2,1,0:T(8,128)(2,1)}), bf16[32,16,2048]{2,1,0:T(8,128)(2,1)}, u32[]{:S(2)}, u32[]{:S(2)}) %all-to-all-start.3) | async-done | bytes 2097184 | tf_op jit(solution)/shard_map/all_to_all | solution.py:153
  212.2 2.3 fusion.20
  214.6 3.5 %fusion.128 = (f32[512,256]{1,0:T(8,128)S(1)}, bf16[512,256]{1,0:T(8,128)(2,1)S(1)}, f32[512,256]{1,0:T(8,128)}, f32[512,256]{1,0:T(8,128)}) fusion(f32[512,256]{1,0:T(8,128)S(1)} %fusion.20, bf16[512,2048]{1,0:T(8,128)(2,1)} %bitcast.56, bf16[1,2048,256]{2,1,0:T(8,128)(2,1)S(1)} %copy-done), kind=kOutput, calls=%fused_computation.231 | convolution fusion | flops 537657344 | bytes 5505024 | tf_op jit(solution)/shard_map/dot_general | solution.py:21
  218.8 1.4 convolution_convert_fusion
  221.0 1.8 copy.148
  222.7 1.7 slice_bitcast_fusion.7
  224.4 1.8 copy.141
  226.2 1.8 copy.150
  228.0 2.5 multiply_reduce_fusion
  231.7 1.7 slice_bitcast_fusion.5
  233.4 1.1 copy.146
  236.7 1.5 pad_maximum_fusion.1
  238.2 4.6 %all-to-all-start.5 = ((bf16[32,8,4224]{2,1,0:T(8,128)(2,1)}), bf16[32,8,4224]{2,1,0:T(8,128)(2,1)S(1)}, u32[]{:S(2)}, u32[]{:S(2)}) async-start(bf16[32,8,4224]{2,1,0:T(8,128)(2,1)} %pad_maximum_fusion.1), calls=%async_computation.5 | async-start | bytes 4325376 | tf_op jit(solution)/shard_map/all_to_all | solution.py:159
  245.7 26.1 %all-to-all-done.5 = bf16[32,8,4224]{2,1,0:T(8,128)(2,1)S(1)} async-done(((bf16[32,8,4224]{2,1,0:T(8,128)(2,1)}), bf16[32,8,4224]{2,1,0:T(8,128)(2,1)S(1)}, u32[]{:S(2)}, u32[]{:S(2)}) %all-to-all-start.5) | async-done | bytes 2162720 | tf_op jit(solution)/shard_map/all_to_all | solution.py:159
  (184 shorter events, 30.0 us)
Async XLA Ops:
  0.6 78.9 %copy-start = (bf16[1,2048,256]{2,1,0:T(8,128)(2,1)S(1)}, bf16[1,2048,256]{2,1,0:T(8,128)(2,1)}, u32[]{:S(2)}) copy-start(bf16[1,2048,256]{2,1,0:T(8,128)(2,1)} %param.22) | copy-start | bytes 3145732
  0.7 11.7 %copy-start.46 = (pred[128]{0:T(512)(128)(4,1)}, pred[128]{0:T(512)(128)(4,1)S(1)}, u32[]{:S(2)}) copy-start(pred[128]{0:T(512)(128)(4,1)S(1)} %iota_compare_fusion.4) | copy-start | bytes 388
  3.9 8.4 %copy-start.15 = (f32[2,2,32,2,64]{4,2,3,1,0:T(8,128)}, f32[2,2,32,2,64]{4,2,3,1,0:T(8,128)S(1)}, u32[]{:S(2)}) copy-start(f32[2,2,32,2,64]{4,2,3,1,0:T(8,128)S(1)} %fusion.84) | copy-start | bytes 196612
  6.1 18.2 %copy-start.42 = (f32[32]{0:T(128)}, f32[32]{0:T(128)S(1)}, u32[]{:S(2)}) copy-start(f32[32]{0:T(128)S(1)} %add_rsqrt_fusion.2) | copy-start | bytes 388
  10.4 2.0 copy-start.48
  12.2 11.7 %copy-start.13 = (bf16[1,32,2048]{2,1,0:T(8,128)(2,1)S(1)}, bf16[1,32,2048]{2,1,0:T(8,128)(2,1)}, u32[]{:S(2)}) copy-start(bf16[1,32,2048]{2,1,0:T(8,128)(2,1)} %param.13) | copy-start | bytes 393220
  12.3 11.7 %copy-start.33 = (f32[1,2048]{1,0:T(1,128)S(1)}, f32[1,2048]{1,0:T(1,128)}, u32[]{:S(2)}) copy-start(f32[1,2048]{1,0:T(1,128)} %param.20) | copy-start | bytes 24580
  12.4 11.9 %copy-start.7 = (bf16[2,1,32,2048]{3,2,1,0:T(8,128)(2,1)S(1)}, bf16[2,1,32,2048]{3,2,1,0:T(8,128)(2,1)}, u32[]{:S(2)}) copy-start(bf16[2,1,32,2048]{3,2,1,0:T(8,128)(2,1)} %param.15) | copy-start | bytes 786436
  13.5 28.2 %all-to-all-start.1 = ((bf16[32,8,2176]{2,1,0:T(8,128)(2,1)}), bf16[32,8,2176]{2,1,0:T(8,128)(2,1)S(1)}, u32[]{:S(2)}, u32[]{:S(2)}) async-start(bf16[32,8,2176]{2,1,0:T(8,128)(2,1)} %bitcast.30), calls=%async_computation.1 | async-start | bytes 2228224 | tf_op jit(solution)/shard_map/all_to_all | solution.py:154
  41.7 6.4 %copy-start.8 = (bf16[32,8,2176]{2,1,0:T(8,128)(2,1)}, bf16[32,8,2176]{2,1,0:T(8,128)(2,1)S(1)}, u32[]{:S(2)}) copy-start(bf16[32,8,2176]{2,1,0:T(8,128)(2,1)S(1)} %all-to-all-done.1) | copy-start | bytes 3342340
  43.3 33.1 %copy-start.1 = (bf16[1,2048,256]{2,1,0:T(8,128)(2,1)S(1)}, bf16[1,2048,256]{2,1,0:T(8,128)(2,1)}, u32[]{:S(2)}) copy-start(bf16[1,2048,256]{2,1,0:T(8,128)(2,1)} %param.23) | copy-start | bytes 3145732
  43.4 33.1 %all-to-all-start = ((bf16[32,16,2048]{2,1,0:T(8,128)(2,1)}), bf16[32,16,2048]{2,1,0:T(8,128)(2,1)}, u32[]{:S(2)}, u32[]{:S(2)}) async-start(bf16[32,16,2048]{2,1,0:T(8,128)(2,1)} %bitcast.15), calls=%async_computation | async-start | bytes 4194304 | tf_op jit(solution)/shard_map/all_to_all | solution.py:153
  82.9 9.4 %copy-start.3 = (bf16[1,256,2048]{2,1,0:T(8,128)(2,1)S(1)}, bf16[1,256,2048]{2,1,0:T(8,128)(2,1)}, u32[]{:S(2)}) copy-start(bf16[1,256,2048]{2,1,0:T(8,128)(2,1)} %param.24) | copy-start | bytes 3145732
  92.3 2.5 copy-start.9
  92.3 2.5 copy-start.34
  95.9 4.0 %copy-start.19 = (f32[256,256]{0,1:T(8,128)S(1)}, f32[256,256]{0,1:T(8,128)}, u32[]{:S(2)}) copy-start(f32[256,256]{0,1:T(8,128)} %get-tuple-element.47) | copy-start | bytes 786436
  95.9 4.0 %copy-start.22 = (f32[256,256]{0,1:T(8,128)S(1)}, f32[256,256]{0,1:T(8,128)}, u32[]{:S(2)}) copy-start(f32[256,256]{0,1:T(8,128)} %copy.129) | copy-start | bytes 786436
  103.7 33.6 %all-to-all-start.2 = ((bf16[32,8,4224]{2,1,0:T(8,128)(2,1)}), bf16[32,8,4224]{2,1,0:T(8,128)(2,1)S(1)}, u32[]{:S(2)}, u32[]{:S(2)}) async-start(bf16[32,8,4224]{2,1,0:T(8,128)(2,1)} %pad_maximum_fusion), calls=%async_computation.2 | async-start | bytes 4325376 | tf_op jit(solution)/shard_map/all_to_all | solution.py:159
  137.3 1.7 copy-start.14
  137.3 2.1 copy-start.41
  137.3 6.0 %copy-start.35 = (bf16[1,32,2048]{2,1,0:T(8,128)(2,1)S(1)}, bf16[1,32,2048]{2,1,0:T(8,128)(2,1)}, u32[]{:S(2)}) copy-start(bf16[1,32,2048]{2,1,0:T(8,128)(2,1)} %param.14) | copy-start | bytes 393220
  137.3 6.2 %copy-start.36 = (bf16[1,2048,8]{1,2,0:T(8,128)(2,1)S(1)}, bf16[1,2048,8]{1,2,0:T(8,128)(2,1)}, u32[]{:S(2)}) copy-start(bf16[1,2048,8]{1,2,0:T(8,128)(2,1)} %param.21) | copy-start | bytes 98308
  137.3 6.4 %copy-start.43 = (f32[32]{0:T(128)S(1)}, f32[32]{0:T(128)}, u32[]{:S(2)}) copy-start(f32[32]{0:T(128)} %copy-done.42) | copy-start | bytes 388
  137.7 7.5 %copy-start.24 = (bf16[1,32,2048]{2,1,0:T(8,128)(2,1)S(1)}, bf16[1,32,2048]{2,1,0:T(8,128)(2,1)}, u32[]{:S(2)}) copy-start(bf16[1,32,2048]{2,1,0:T(8,128)(2,1)} %param.16) | copy-start | bytes 393220
  137.7 9.0 %copy-start.47 = (pred[128]{0:T(512)(128)(4,1)S(1)}, pred[128]{0:T(512)(128)(4,1)}, u32[]{:S(2)}) copy-start(pred[128]{0:T(512)(128)(4,1)} %copy-done.46) | copy-start | bytes 388
  137.7 9.0 %copy-start.49 = (bf16[128]{0:T(256)(128)(2,1)S(1)}, bf16[128]{0:T(256)(128)(2,1)}, u32[]{:S(2)}) copy-start(bf16[128]{0:T(256)(128)(2,1)} %copy-done.48) | copy-start | bytes 772
  137.7 14.1 %copy-start.25 = (bf16[1,32,2048]{2,1,0:T(8,128)(2,1)S(1)}, bf16[1,32,2048]{2,1,0:T(8,128)(2,1)}, u32[]{:S(2)}) copy-start(bf16[1,32,2048]{2,1,0:T(8,128)(2,1)} %param.17) | copy-start | bytes 393220
  139.4 4.4 %copy-start.29 = (bf16[32,2048]{1,0:T(8,128)(2,1)}, bf16[32,2048]{1,0:T(8,128)(2,1)S(1)}, u32[]{:S(2)}) copy-start(bf16[32,2048]{1,0:T(8,128)(2,1)S(1)} %fusion.10) | copy-start | bytes 393220
  139.8 3.5 %collective-permute-start = (bf16[32,2048]{1,0:T(8,128)(2,1)S(1)}, bf16[32,2048]{1,0:T(8,128)(2,1)S(1)}, u32[]{:S(2)}, u32[]{:S(2)}) collective-permute-start(bf16[32,2048]{1,0:T(8,128)(2,1)S(1)} %fusion.10), channel_id=1, source_target_pairs={{0,32},{32,64},{64,96},{96,128},{128,160},{160,192},{192,224},{224... | collective-permute-start | bytes 393224 | tf_op jit(solution)/shard_map/ppermute | solution.py:14
  143.5 16.3 %copy-start.11 = (bf16[32,2048]{1,0:T(8,128)(2,1)}, bf16[32,2048]{1,0:T(8,128)(2,1)S(1)}, u32[]{:S(2)}) copy-start(bf16[32,2048]{1,0:T(8,128)(2,1)S(1)} %get-tuple-element.28) | copy-start | bytes 393220
  144.3 15.8 %copy-start.44 = (f32[32]{0:T(128)}, f32[32]{0:T(128)S(1)}, u32[]{:S(2)}) copy-start(f32[32]{0:T(128)S(1)} %add_rsqrt_fusion) | copy-start | bytes 388
  145.3 6.4 %collective-permute-start.1 = (bf16[32,2048]{1,0:T(8,128)(2,1)S(1)}, bf16[32,2048]{1,0:T(8,128)(2,1)S(1)}, u32[]{:S(2)}, u32[]{:S(2)}) collective-permute-start(bf16[32,2048]{1,0:T(8,128)(2,1)S(1)} %fusion.57), channel_id=1, source_target_pairs={{32,0},{64,32},{96,64},{128,96},{160,128},{192,160},{224,192},{256... | collective-permute-start | bytes 393224 | tf_op jit(solution)/shard_map/ppermute | solution.py:14
  153.5 24.0 %all-to-all-start.4 = ((bf16[32,8,2176]{2,1,0:T(8,128)(2,1)}), bf16[32,8,2176]{2,1,0:T(8,128)(2,1)S(1)}, u32[]{:S(2)}, u32[]{:S(2)}) async-start(bf16[32,8,2176]{2,1,0:T(8,128)(2,1)} %bitcast.65), calls=%async_computation.4 | async-start | bytes 2228224 | tf_op jit(solution)/shard_map/all_to_all | solution.py:154
  177.5 6.5 %copy-start.10 = (bf16[32,8,2176]{2,1,0:T(8,128)(2,1)}, bf16[32,8,2176]{2,1,0:T(8,128)(2,1)S(1)}, u32[]{:S(2)}) copy-start(bf16[32,8,2176]{2,1,0:T(8,128)(2,1)S(1)} %all-to-all-done.4) | copy-start | bytes 3342340
  179.1 33.1 %copy-start.2 = (bf16[1,2048,256]{2,1,0:T(8,128)(2,1)S(1)}, bf16[1,2048,256]{2,1,0:T(8,128)(2,1)}, u32[]{:S(2)}) copy-start(bf16[1,2048,256]{2,1,0:T(8,128)(2,1)} %param.23) | copy-start | bytes 3145732
  179.2 33.1 %all-to-all-start.3 = ((bf16[32,16,2048]{2,1,0:T(8,128)(2,1)}), bf16[32,16,2048]{2,1,0:T(8,128)(2,1)}, u32[]{:S(2)}, u32[]{:S(2)}) async-start(bf16[32,16,2048]{2,1,0:T(8,128)(2,1)} %bitcast.55), calls=%async_computation.3 | async-start | bytes 4194304 | tf_op jit(solution)/shard_map/all_to_all | solution.py:153
  214.5 3.5 %copy-start.38 = (f32[512,256]{1,0:T(8,128)}, f32[512,256]{1,0:T(8,128)S(1)}, u32[]{:S(2)}) copy-start(f32[512,256]{1,0:T(8,128)S(1)} %fusion.20) | copy-start | bytes 1572868
  214.6 4.2 %copy-start.4 = (bf16[1,256,2048]{2,1,0:T(8,128)(2,1)S(1)}, bf16[1,256,2048]{2,1,0:T(8,128)(2,1)}, u32[]{:S(2)}) copy-start(bf16[1,256,2048]{2,1,0:T(8,128)(2,1)} %param.24) | copy-start | bytes 3145732
  230.4 4.0 %copy-start.18 = (f32[256,256]{0,1:T(8,128)S(1)}, f32[256,256]{0,1:T(8,128)}, u32[]{:S(2)}) copy-start(f32[256,256]{0,1:T(8,128)} %get-tuple-element.51) | copy-start | bytes 786436
  230.4 4.0 %copy-start.23 = (f32[256,256]{0,1:T(8,128)S(1)}, f32[256,256]{0,1:T(8,128)}, u32[]{:S(2)}) copy-start(f32[256,256]{0,1:T(8,128)} %copy.141) | copy-start | bytes 786436
  238.2 33.7 %all-to-all-start.5 = ((bf16[32,8,4224]{2,1,0:T(8,128)(2,1)}), bf16[32,8,4224]{2,1,0:T(8,128)(2,1)S(1)}, u32[]{:S(2)}, u32[]{:S(2)}) async-start(bf16[32,8,4224]{2,1,0:T(8,128)(2,1)} %pad_maximum_fusion.1), calls=%async_computation.5 | async-start | bytes 4325376 | tf_op jit(solution)/shard_map/all_to_all | solution.py:159
  245.7 28.6 %copy-start.37 = (bf16[1,2048,8]{1,2,0:T(8,128)(2,1)S(1)}, bf16[1,2048,8]{1,2,0:T(8,128)(2,1)}, u32[]{:S(2)}) copy-start(bf16[1,2048,8]{1,2,0:T(8,128)(2,1)} %param.21) | copy-start | bytes 98308
  271.8 2.1 copy-start.40
  271.8 2.5 copy-start.45
  271.8 2.9 %copy-start.26 = (bf16[1,32,2048]{2,1,0:T(8,128)(2,1)S(1)}, bf16[1,32,2048]{2,1,0:T(8,128)(2,1)}, u32[]{:S(2)}) copy-start(bf16[1,32,2048]{2,1,0:T(8,128)(2,1)} %param.17) | copy-start | bytes 393220
  271.9 2.9 %copy-start.28 = (bf16[32,2048]{1,0:T(8,128)(2,1)S(1)}, bf16[32,2048]{1,0:T(8,128)(2,1)}, u32[]{:S(2)}) copy-start(bf16[32,2048]{1,0:T(8,128)(2,1)} %copy-done.27) | copy-start | bytes 393220
  272.2 2.8 copy-start.30
  272.2 2.8 copy-start.32
  (10 other events, 10.7 us)

commit v2 on v1

--- a/solution.py
+++ b/solution.py
@@ -1,6 +1,10 @@
+import functools
+
 import jax
 import jax.numpy as jnp
 from jax import lax
+from jax.experimental import pallas as pl
+from jax.experimental.pallas import tpu as pltpu
 from jax.sharding import PartitionSpec as P
 
 SPLIT = 4
@@ -14,40 +18,262 @@
     return lax.ppermute(block, axis, route)
 
 
-def expert_work(rows, carried, gate_q, up_q, down_q, capacity):
-    sources, pair_rows, width = rows.shape
-    hidden_q = gate_q.shape[1]
-    flat = rows.reshape(sources * pair_rows, width)
-    pre_gate = jnp.dot(flat, gate_q, preferred_element_type=jnp.float32)
-    pre_up = jnp.dot(flat, up_q, preferred_element_type=jnp.float32)
-    sigmoid_g = jax.nn.sigmoid(pre_gate)
-    activated = pre_gate * sigmoid_g
-    hidden = (activated * pre_up).astype(jnp.bfloat16)
-
-    def half(value, which):
-        paired = value.reshape(sources, 2, capacity, hidden_q)
-        return paired[:, which].reshape(sources * capacity, hidden_q)
-
-    y_part = jnp.dot(half(hidden, 0), down_q, preferred_element_type=jnp.float32)
+MESH = pl.DeviceIdType.MESH
+SIDE = 4
+CHIPS = SIDE * SIDE
+
+
+class Place:
+    def __init__(self):
+        self.section = lax.axis_index("section")
+        me = lax.axis_index("expert")
+        self.chip = me // 2
+        self.core = me % 2
+
+    def away(self, step, sign):
+        x = (self.chip // SIDE + sign * (step // SIDE) + SIDE) % SIDE
+        y = (self.chip % SIDE + sign * (step % SIDE) + SIDE) % SIDE
+        return x * SIDE + y
+
+    def same_core(self, chip):
+        return (self.section, chip * 2 + self.core)
+
+    def other_core(self):
+        return (self.section, self.chip * 2 + 1 - self.core)
+
+    def greet(self):
+        barrier = pltpu.get_barrier_semaphore()
+
+        def signal(step, carry):
+            pl.semaphore_signal(
+                barrier,
+                inc=1,
+                device_id=self.same_core(self.away(step, 1)),
+                device_id_type=MESH,
+            )
+            return carry
+
+        lax.fori_loop(1, CHIPS, signal, 0)
+        pl.semaphore_signal(
+            barrier, inc=1, device_id=self.other_core(), device_id_type=MESH
+        )
+        pl.semaphore_wait(barrier, CHIPS)
+
+
+def steps_of(first, body):
+    def step_once(step, carry):
+        body(step)
+        return carry
+
+    lax.fori_loop(first, CHIPS, step_once, 0)
+
+
+def remote(src, dst, send, recv, device):
+    return pltpu.make_async_remote_copy(
+        src_ref=src,
+        dst_ref=dst,
+        send_sem=send,
+        recv_sem=recv,
+        device_id=device,
+        device_id_type=MESH,
+    )
+
+
+def dispatch_kernel(number, *refs):
+    sources, results = refs[:number], refs[number : 2 * number]
+    send, recv, pass_send, pass_recv, own = refs[2 * number :]
+    at = Place()
+    at.greet()
+    streams = range(number)
+
+    def outward(i, step):
+        goal = at.away(step, 1)
+        return remote(
+            sources[i].at[goal // 2],
+            results[i].at[at.core * CHIPS + at.chip],
+            send.at[i, step],
+            recv.at[i, step],
+            at.same_core(goal),
+        )
+
+    def passed(i, step):
+        slot = at.core * CHIPS + at.away(step, -1)
+        return remote(
+            results[i].at[slot],
+            results[i].at[slot],
+            pass_send.at[i, step],
+            pass_recv.at[i, step],
+            at.other_core(),
+        )
+
+    def own_copy(i):
+        return pltpu.make_async_copy(
+            sources[i].at[at.chip // 2], results[i].at[at.core * CHIPS + at.chip], own.at[i]
+        )
+
+    def start(step):
+        for i in streams:
+            outward(i, step).start()
+
+    def hand_over(step):
+        for i in streams:
+            outward(i, step).wait_recv()
+            passed(i, step).start()
+
+    def finish(step):
+        for i in streams:
+            passed(i, step).wait_send()
+            passed(i, step).wait_recv()
+
+    def sent(step):
+        for i in streams:
+            outward(i, step).wait_send()
+
+    for i in streams:
+        own_copy(i).start()
+    steps_of(1, start)
+    for i in streams:
+        own_copy(i).wait()
+        passed(i, 0).start()
+    steps_of(1, hand_over)
+    steps_of(1, sent)
+    steps_of(0, finish)
+
+
+def collect_kernel(number, *refs):
+    parts, results = refs[:number], refs[number : 2 * number]
+    arrived, joined = refs[2 * number : 3 * number], refs[3 * number : 4 * number]
+    send, recv, pass_send, pass_recv = refs[4 * number :]
+    at = Place()
+    at.greet()
+    streams = range(number)
+
+    def passed(i, step):
+        goal = at.away(step, 1)
+        return remote(
+            parts[i].at[(1 - at.core) * CHIPS + goal],
+            arrived[i].at[goal],
+            pass_send.at[i, step],
+            pass_recv.at[i, step],
+            at.other_core(),
+        )
+
+    def outward(i, step):
+        goal = at.away(step, 1)
+        return remote(
+            joined[i].at[goal],
+            results[i].at[at.chip],
+            send.at[i, step],
+            recv.at[i, step],
+            at.same_core(goal),
+        )
+
+    def added(i, step):
+        passed(i, step).wait_recv()
+        goal = at.away(step, 1)
+        total = parts[i][at.core * CHIPS + goal].astype(jnp.float32) + arrived[i][goal].astype(
+            jnp.float32
+        )
+        return goal, total.astype(jnp.bfloat16)
+
+    def start(step):
+        for i in streams:
+            passed(i, step).start()
+
+    def send_on(step):
+        for i in streams:
+            goal, total = added(i, step)
+            joined[i][goal] = total
+            outward(i, step).start()
+
+    def finish(step):
+        for i in streams:
+            outward(i, step).wait_send()
+            outward(i, step).wait_recv()
+
+    def sent(step):
+        for i in streams:
+            passed(i, step).wait_send()
+
+    steps_of(1, start)
+    for i in streams:
+        passed(i, 0).start()
+    steps_of(1, send_on)
+    for i in streams:
+        goal, total = added(i, 0)
+        results[i][goal] = total
+    steps_of(0, sent)
+    steps_of(1, finish)
+
+
+def dispatch_rows(arrays):
+    number = len(arrays)
+    whole = pl.BlockSpec(memory_space=pltpu.VMEM)
+    sems = pltpu.SemaphoreType.DMA
+    return pl.pallas_call(
+        functools.partial(dispatch_kernel, number),
+        out_shape=[jax.ShapeDtypeStruct((2 * CHIPS,) + a.shape[1:], a.dtype) for a in arrays],
+        in_specs=[whole] * number,
+        out_specs=[whole] * number,
+        scratch_shapes=[sems((number, CHIPS))] * 4 + [sems((number,))],
+        compiler_params=pltpu.CompilerParams(
+            collective_id=0, has_side_effects=True, vmem_limit_bytes=32 * 2**20
+        ),
+        name="dispatch_rows",
+    )(*arrays)
+
+
+def collect_rows(arrays):
+    number = len(arrays)
+    whole = pl.BlockSpec(memory_space=pltpu.VMEM)
+    sems = pltpu.SemaphoreType.DMA
+    blocks = [(CHIPS,) + a.shape[1:] for a in arrays]
+    return pl.pallas_call(
+        functools.partial(collect_kernel, number),
+        out_shape=[jax.ShapeDtypeStruct(s, a.dtype) for s, a in zip(blocks, arrays)],
+        in_specs=[whole] * number,
+        out_specs=[whole] * number,
+        scratch_shapes=[pltpu.VMEM(s, a.dtype) for s, a in zip(blocks, arrays)] * 2
+        + [sems((number, CHIPS))] * 4,
+        compiler_params=pltpu.CompilerParams(
+            collective_id=1, has_side_effects=True, vmem_limit_bytes=32 * 2**20
+        ),
+        name="collect_rows",
+    )(*arrays)
+
+
+def expert_work(rows_f, rows_b, carried, gate_q, up_q, down_q):
+    sources, capacity, width = rows_f.shape
+
+    def first(rows):
+        flat = rows.reshape(sources * capacity, width)
+        pre_gate = jnp.dot(flat, gate_q, preferred_element_type=jnp.float32)
+        pre_up = jnp.dot(flat, up_q, preferred_element_type=jnp.float32)
+        sigmoid_g = jax.nn.sigmoid(pre_gate)
+        activated = pre_gate * sigmoid_g
+        hidden = (activated * pre_up).astype(jnp.bfloat16)
+        return pre_gate, pre_up, sigmoid_g, activated, hidden
+
+    hidden_f = first(rows_f)[-1]
+    pre_gate, pre_up, sigmoid_g, activated, hidden_b = first(rows_b)
+    y_part = jnp.dot(hidden_f, down_q, preferred_element_type=jnp.float32).astype(jnp.bfloat16)
     grads = carried[:, :, :width].reshape(sources * capacity, width)
     scales = carried[:, :, width].reshape(sources * capacity, 1).astype(jnp.float32)
     plain_h = jnp.dot(grads, down_q.T, preferred_element_type=jnp.float32)
-    inner_dot = jnp.sum(plain_h * half(hidden, 1).astype(jnp.float32), axis=-1, keepdims=True)
+    inner_dot = jnp.sum(plain_h * hidden_b.astype(jnp.float32), axis=-1, keepdims=True)
     back_h = plain_h * scales
-    slope_g = half(sigmoid_g, 1)
-    d_gate = back_h * half(pre_up, 1) * slope_g * (1.0 + half(pre_gate, 1) * (1.0 - slope_g))
-    d_up = back_h * half(activated, 1)
+    d_gate = back_h * pre_up * sigmoid_g * (1.0 + pre_gate * (1.0 - sigmoid_g))
+    d_up = back_h * activated
     dn_part = jnp.dot(
         d_gate.astype(jnp.bfloat16), gate_q.T, preferred_element_type=jnp.float32
     ) + jnp.dot(d_up.astype(jnp.bfloat16), up_q.T, preferred_element_type=jnp.float32)
-    dots = jnp.broadcast_to(inner_dot, (sources * capacity, LANES))
-    joined = jnp.concatenate([y_part, dn_part, dots], axis=-1).astype(jnp.bfloat16)
-    return joined.reshape(sources, capacity, 2 * width + LANES)
-
-
-def spread(block, experts):
-    repeated = jnp.broadcast_to(block[:, None], (experts, SPLIT) + block.shape[1:])
-    return repeated.reshape((experts * SPLIT,) + block.shape[1:])
+    dots = jnp.broadcast_to(inner_dot, (sources * capacity, LANES)).astype(jnp.bfloat16)
+    shape = (sources, capacity)
+    return (
+        y_part.reshape(shape + (width,)),
+        dn_part.astype(jnp.bfloat16).reshape(shape + (width,)),
+        dots.reshape(shape + (LANES,)),
+    )
 
 
 def on_device(
@@ -135,13 +361,6 @@
         unit_f, _ = norm_of(forward_x)
         normed_f = (unit_f * gain_row).astype(bf16)
         gate_f = jax.nn.softplus(picked_of(normed_f, 0, k)) * live[0, k]
-        rows = jnp.concatenate(
-            [
-                placed(0, k, normed_f).reshape(experts, capacity, width),
-                rows_b.reshape(experts, capacity, width),
-            ],
-            axis=1,
-        )
         lane = jnp.arange(LANES)
         extra = jnp.where(
             lane == 0,
@@ -150,26 +369,29 @@
         ).astype(bf16)
         carried = jnp.concatenate([placed(1, k, cotangent), extra], axis=1)
         carried = carried.reshape(experts, capacity, width + LANES)
-        got_rows = lax.all_to_all(spread(rows, experts), "expert", 0, 0, tiled=True)
-        got_carried = lax.all_to_all(spread(carried, experts), "expert", 0, 0, tiled=True)
+        grouped = (experts, capacity, width)
+        got_f, got_b, got_carried = dispatch_rows(
+            [placed(0, k, normed_f).reshape(grouped), rows_b.reshape(grouped), carried]
+        )
         if totals is None:
             seen = got_carried[:, 0, width + 1 : width + 1 + TICKS].astype(f32)
             totals = jnp.sum(seen, axis=0)
-        partial = expert_work(got_rows, got_carried, gate_cols, up_cols, down_rows, capacity)
-        back = lax.all_to_all(partial, "expert", 0, 0, tiled=True)
-        summed = jnp.sum(
-            back.astype(f32).reshape(experts, SPLIT, capacity, 2 * width + LANES), axis=1
-        ).reshape(slots, 2 * width + LANES)
+        partial = expert_work(got_f, got_b, got_carried, gate_cols, up_cols, down_rows)
+        halves = [
+            jnp.sum(part.astype(f32).reshape(experts, 2, capacity, -1), axis=1).reshape(slots, -1)
+            for part in collect_rows(partial)
+        ]
+        y_sum, dn_sum, dot_sum = halves
         combine_f = jnp.sum(table[0, k] * gate_f[:, :, None], axis=1)
         out_f = forward_x.astype(f32) + jnp.dot(
-            combine_f, summed[:, :width], precision=lax.Precision.HIGHEST
-        )
-        dots = jnp.sum(table[1, k] * summed[:, 2 * width], axis=-1)
+            combine_f, y_sum, precision=lax.Precision.HIGHEST
+        )
+        dots = jnp.sum(table[1, k] * dot_sum[:, 0], axis=-1)
         dpick = (dots + weight) * jax.nn.sigmoid(picked_b) * live[1, k]
         dlogit = jnp.sum(chosen[1, k] * dpick[:, :, None], axis=1)
         dnorm = jnp.dot(
             jnp.sum(table[1, k], axis=1),
-            summed[:, width : 2 * width],
+            dn_sum,
             precision=lax.Precision.HIGHEST,
         ) + jnp.dot(dlogit, router_t, precision=lax.Precision.HIGHEST)
         scaled = dnorm * gain_row

time: 281 us -> 183 us (0.65)
  waiting for transfers between devices: 149 us -> 3.86 us
  Pallas kernels: 0 us -> 114 us
  starting transfers between devices: 38.3 us -> 5.16 us
  local copies, waits for them, and re-layouts: 36.9 us -> 7.36 us
  other arithmetic: 19.3 us -> 12.8 us
  matrix products: 28.6 us -> 32.3 us
    all_to_all x6 -> x0, waiting for transfers between devices: 142 us -> none  [the longest x2 54.9 us: on_device(): got_rows = lax.all_to_all(spread(rows, experts), 'expert', 0, 0, tiled=True)]
    pallas_call x0 -> x4, Pallas kernels: none -> 114 us  [the longest x2 64.9 us: dispatch_rows(): pl.pallas_call(functools.partial(dispatch_kernel, number), out_shape=[jax...]
    all_to_all x6 -> x0, starting transfers between devices: 35.4 us -> none  [the longest x2 16.7 us: on_device(): lax.all_to_all(spread(carried, experts), 'expert', 0, 0, tiled=True)]
    another operation x18 -> x0, local copies, waits for them, and re-layouts: 19.9 us -> none  [the longest x16 19.7 us: half(): return paired[:, which].reshape(sources * capacity, hidden_q)]
    broadcast_in_dim x6 -> x2, local copies, waits for them, and re-layouts: 5.66 us -> 0.19 us  [expert_work(): jnp.broadcast_to(inner_dot, (sources * capacity, LANES))]
    concatenate x4 -> x0, other arithmetic: 3.13 us -> none  [the longest x2 3.04 us: expert_work(): jnp.concatenate([y_part, dn_part, dots], axis=-1).astype(jnp.bfloat16)]
    ppermute x2, waiting for transfers between devices: 6.94 us -> 3.86 us  [from_behind(): return lax.ppermute(block, axis, route)]
    dot_general x2, matrix products: 1.01 us -> 3.93 us  [expert_work(): jnp.dot(d_gate.astype(jnp.bfloat16), gate_q.T, preferred_element_type=jnp...]
  transfers between devices with their start and end apart: 8 -> 2, of which waited for: 8 -> 1; matrix products, arithmetic and copies ran while one was open for 2% -> 2% of each run, Pallas kernels for 0% -> 0%
where the time goes in v2:
time: 183 us; the launch traced here: 180 us
  Pallas kernels  114 us (62%)
  matrix products  32.3 us (18%)
  other arithmetic  12.8 us (7%)
  local copies, waits for them, and re-layouts  7.36 us (4%)
  starting transfers between devices  5.16 us (3%)
  between operations  4.82 us (3%)
  waiting for transfers between devices  3.86 us (2%)
    pallas_call x2, Pallas kernels, dispatch_rows(): pl.pallas_call(functools.partial(dispatch_kernel, number), out_shape=[jax...  64.9 us
    pallas_call x2, Pallas kernels, collect_rows(): pl.pallas_call(functools.partial(collect_kernel, number), out_shape=[jax....  49 us
    dot_general x4, matrix products, first(): pre_gate = jnp.dot(flat, gate_q, preferred_element_type=jnp.float32)  6.47 us
    dot_general x2, matrix products, expert_work(): jnp.dot(hidden_f, down_q, preferred_element_type=jnp.float32)  5.19 us
    ppermute x2, starting transfers between devices, from_behind(): return lax.ppermute(block, axis, route)  5.16 us
    unnamed x97, local copies, waits for them, and re-layouts  4.37 us
    dot_general x2, matrix products, expert_work(): plain_h = jnp.dot(grads, down_q.T, preferred_element_type=jnp.float32)  4.21 us
    dot_general x6, matrix products, placed(): lax.dot_general(dispatch[m, k], rows, (((0,), (0,)), ((), ())), preferred...  4.13 us
  transfers between devices with their start and end apart: 2, of which 1 were waited for; matrix products, arithmetic and copies ran while one was open for 2% of the time, Pallas kernels for 0%

profile of v2, /device:TPU:1, one launch (start us, length us, event | category | flops | bytes accessed | tf_op | source)
XLA Modules:
  0.0 180.2 jit_solution(13658196178976548562)
XLA Ops:
  0.7 0.9 slice_reduce_fusion.4
  1.6 0.7 fusion.173
  2.3 0.8 copy.103
  4.0 1.1 fusion.94
  5.1 1.0 fusion.88
  6.1 1.1 fusion.149
  7.3 1.1 fusion.131
  8.4 1.2 fusion.6.refs_0_
  9.6 1.9 %fusion.7.refs_1_ = bf16[8,8,2048]{2,1,0:T(8,128)(2,1)} fusion(f32[2048]{0:T(1024)} %bitcast.350, f32[32]{0:T(128)S(1)} %add_rsqrt_fusion.2, bf16[2,1,32,2048]{3,2,1,0:T(8,128)(2,1)} %param.15, bf16[2,2,32,64]{3,2,1,0:T(8,128)(2,1)S(1)} %fusion.129), kind=kOutput, calls=%fused_computation.17 | convolution fusion | flops 8781824 | bytes 410112 | tf_op jit(solution)/shard_map/dot_general | solution.py:335
  11.5 0.6 fusion.175
  12.5 1.3 compare_select_fusion.5
  13.8 0.6 fusion.163
  14.7 0.9 copy-done.1
  15.6 32.9 %dispatch_rows.2 = (bf16[32,8,2048]{2,1,0:T(8,128)(2,1)S(1)}, bf16[32,8,2048]{2,1,0:T(8,128)(2,1)S(1)}, bf16[32,8,2176]{2,1,0:T(8,128)(2,1)S(1)}) custom-call(bf16[8,8,2048]{2,1,0:T(8,128)(2,1)S(1)} %fusion.6.refs_0_, bf16[8,8,2048]{2,1,0:T(8,128)(2,1)S(1)} %copy-done.1, bf16[8,8,2176]{2,1,0:T(8,128)(2,1)S(1)} %maximum_bitcast_fusion.refs_2_), custom_call_target="tpu_custom_call" | custom-call | tf_op jit(solution)/shard_map/dispatch_rows/pallas_call | solution.py:213
  48.5 1.0 copy-done.4
  49.7 1.8 %fusion.26 = f32[256,256]{1,0:T(8,128)S(1)} fusion(bf16[32,8,2048]{2,1,0:T(8,128)(2,1)S(1)} %get-tuple-element.17, bf16[1,2048,256]{2,1,0:T(8,128)(2,1)} %param.22), kind=kOutput, calls=%fused_computation.46 | convolution fusion | flops 268435456 | bytes 2359296 | tf_op jit(solution)/shard_map/dot_general | solution.py:250
  51.5 0.4 fusion.28
  52.0 1.7 multiply_reduce_fusion.1
  53.7 0.7 convert_element_type.240
  54.4 1.1 fusion.49
  55.6 2.6 %fusion.2.refs_0_ = bf16[32,8,2048]{2,1,0:T(8,128)(2,1)S(1)} fusion(bf16[1,256,2048]{2,1,0:T(8,128)(2,1)} %param.24, bf16[1,2048,256]{2,1,0:T(8,128)(2,1)S(1)} %copy-done, bf16[32,8,2048]{2,1,0:T(8,128)(2,1)S(1)} %get-tuple-element.15, f32[256,256]{1,0:T(8,128)} %fusion.49), kind=kOutput, calls=%fused_computation.6 | convolution fusion | flops 537788416 | bytes 4456448 | tf_op jit(solution)/shard_map/dot_general | solution.py:259
  58.2 1.9 %fusion.46 = f32[256,2048]{1,0:T(8,128)S(1)} fusion(bf16[1,2048,256]{2,1,0:T(8,128)(2,1)} %param.22, f32[256,256]{1,0:T(8,128)S(1)} %fusion.26, f32[256,256]{1,0:T(8,128)} %copy-done.17, f32[256,256]{1,0:T(8,128)} %get-tuple-element.64, f32[256]{0:T(256)S(1)} %reshape.456), kind=kOutput, calls=%fused_computation.66 | convolution fusion | flops 269156352 | bytes 3933184 | tf_op jit(solution)/shard_map/dot_general | solution.py:267
  60.1 0.5 fusion.5.refs_1_
  60.8 25.5 %collect_rows.2 = (bf16[16,8,2048]{2,1,0:T(8,128)(2,1)S(1)}, bf16[16,8,2048]{2,1,0:T(8,128)(2,1)S(1)}, bf16[16,8,128]{2,1,0:T(8,128)(2,1)S(1)}) custom-call(bf16[32,8,2048]{2,1,0:T(8,128)(2,1)S(1)} %fusion.2.refs_0_, bf16[32,8,2048]{2,1,0:T(8,128)(2,1)S(1)} %fusion.5.refs_1_, bf16[32,8,128]{2,1,0:T(8,128)(2,1)S(1)} %broadcast_in_dim.89.refs_2_), custom_call_target="tpu_custom_call" | custom-call | tf_op jit(solution)/shard_map/collect_rows/pallas_call | solution.py:231
  86.2 0.8 copy-done.2
  87.8 3.7 %collective-permute-start = (bf16[32,2048]{1,0:T(8,128)(2,1)S(1)}, bf16[32,2048]{1,0:T(8,128)(2,1)S(1)}, u32[]{:S(2)}, u32[]{:S(2)}) collective-permute-start(bf16[32,2048]{1,0:T(8,128)(2,1)S(1)} %fusion.12), channel_id=1, source_target_pairs={{0,32},{32,64},{64,96},{96,128},{128,160},{160,192},{192,224},{224... | collective-permute-start | bytes 393224 | tf_op jit(solution)/shard_map/ppermute | solution.py:18
  91.5 0.6 slice_reduce_fusion.2
  92.2 1.0 convert_reduce_fusion.9
  93.8 0.6 fusion.174
  96.8 1.2 fusion.83
  98.2 0.6 fusion.165
  98.9 0.7 select_convert_fusion
  99.8 1.5 collective-permute-start.1
  101.8 3.9 %collective-permute-done.1 = bf16[32,2048]{1,0:T(8,128)(2,1)S(1)} collective-permute-done((bf16[32,2048]{1,0:T(8,128)(2,1)S(1)}, bf16[32,2048]{1,0:T(8,128)(2,1)S(1)}, u32[]{:S(2)}, u32[]{:S(2)}) %collective-permute-start.1) | collective-permute-done | bytes 131104 | tf_op jit(solution)/shard_map/ppermute | solution.py:18
  105.7 0.6 copy-done.27
  106.7 32.1 %dispatch_rows.3 = (bf16[32,8,2048]{2,1,0:T(8,128)(2,1)S(1)}, bf16[32,8,2048]{2,1,0:T(8,128)(2,1)S(1)}, bf16[32,8,2176]{2,1,0:T(8,128)(2,1)S(1)}) custom-call(bf16[8,8,2048]{2,1,0:T(8,128)(2,1)S(1)} %fusion.8.refs_0_, bf16[8,8,2048]{2,1,0:T(8,128)(2,1)S(1)} %fusion.9.refs_1_, bf16[8,8,2176]{2,1,0:T(8,128)(2,1)S(1)} %maximum_bitcast_fusion.1.refs_2_), custom_call_target="tpu_custom_call" | custom-call | tf_op jit(solution)/shard_map/dispatch_rows/pallas_call | solution.py:213
  138.7 1.1 fusion.17
  139.9 1.1 fusion.19
  141.2 2.5 %multiply_reduce_fusion = (bf16[256]{0:T(256)(128)(2,1)S(1)}, f32[256,256]{1,0:T(8,128)}) fusion(f32[256,256]{1,0:T(8,128)} %fusion.19, f32[256,256]{1,0:T(8,128)} %fusion.17, bf16[1,256,2048]{2,1,0:T(8,128)(2,1)} %param.24, bf16[32,8,2176]{2,1,0:T(8,128)(2,1)S(1)} %get-tuple-element.22), kind=kOutput, calls=%fused_computation.124 | convolution fusion | flops 269025024 | bytes 2884096 | tf_op jit(solution)/shard_map/dot_general | solution.py:262
  143.8 2.4 %fusion.24 = f32[256,256]{1,0:T(8,128)} fusion(bf16[32,8,2048]{2,1,0:T(8,128)(2,1)S(1)} %get-tuple-element.21, bf16[1,2048,256]{2,1,0:T(8,128)(2,1)} %param.22), kind=kOutput, calls=%fused_computation.44 | convolution fusion | flops 268435456 | bytes 2359296 | tf_op jit(solution)/shard_map/dot_general | solution.py:250
  146.2 2.6 %fusion.3.refs_0_ = bf16[32,8,2048]{2,1,0:T(8,128)(2,1)S(1)} fusion(bf16[1,256,2048]{2,1,0:T(8,128)(2,1)} %param.24, bf16[32,8,2048]{2,1,0:T(8,128)(2,1)S(1)} %get-tuple-element.21, bf16[1,2048,256]{2,1,0:T(8,128)(2,1)S(1)} %copy-done, f32[256,256]{1,0:T(8,128)} %fusion.24), kind=kOutput, calls=%fused_computation.7 | convolution fusion | flops 537788416 | bytes 4456448 | tf_op jit(solution)/shard_map/dot_general | solution.py:259
  148.8 2.0 %fusion.42 = f32[256,2048]{1,0:T(8,128)S(1)} fusion(bf16[1,2048,256]{2,1,0:T(8,128)(2,1)} %param.22, f32[256,256]{1,0:T(8,128)} %fusion.17, f32[256,256]{1,0:T(8,128)} %fusion.19, f32[256,256]{1,0:T(8,128)} %get-tuple-element.67, f32[256]{0:T(256)S(1)} %reshape.464), kind=kOutput, calls=%fused_computation.62 | convolution fusion | flops 269156352 | bytes 3933184 | tf_op jit(solution)/shard_map/dot_general | solution.py:267
  150.9 0.5 fusion.4.refs_1_
  151.5 23.5 %collect_rows.3 = (bf16[16,8,2048]{2,1,0:T(8,128)(2,1)S(1)}, bf16[16,8,2048]{2,1,0:T(8,128)(2,1)S(1)}, bf16[16,8,128]{2,1,0:T(8,128)(2,1)S(1)}) custom-call(bf16[32,8,2048]{2,1,0:T(8,128)(2,1)S(1)} %fusion.3.refs_0_, bf16[32,8,2048]{2,1,0:T(8,128)(2,1)S(1)} %fusion.4.refs_1_, bf16[32,8,128]{2,1,0:T(8,128)(2,1)S(1)} %broadcast_in_dim.91.refs_2_), custom_call_target="tpu_custom_call" | custom-call | tf_op jit(solution)/shard_map/collect_rows/pallas_call | solution.py:231
  175.3 0.7 multiply_reduce_fusion.2
  176.6 0.4 fusion.78
  177.6 0.7 maximum_bitcast_fusion.3
  178.4 0.7 maximum_bitcast_fusion.2
  (150 shorter events, 6.5 us)
Async XLA Ops:
  0.6 50.9 %copy-start = (bf16[1,2048,256]{2,1,0:T(8,128)(2,1)S(1)}, bf16[1,2048,256]{2,1,0:T(8,128)(2,1)}, u32[]{:S(2)}) copy-start(bf16[1,2048,256]{2,1,0:T(8,128)(2,1)} %param.23) | copy-start | bytes 3145732
  0.6 11.5 %copy-start.19 = (bf16[1,32,2048]{2,1,0:T(8,128)(2,1)S(1)}, bf16[1,32,2048]{2,1,0:T(8,128)(2,1)}, u32[]{:S(2)}) copy-start(bf16[1,32,2048]{2,1,0:T(8,128)(2,1)} %param.16) | copy-start | bytes 393220
  0.7 13.9 %copy-start.46 = (pred[128]{0:T(512)(128)(4,1)}, pred[128]{0:T(512)(128)(4,1)S(1)}, u32[]{:S(2)}) copy-start(pred[128]{0:T(512)(128)(4,1)S(1)} %iota_compare_fusion.4) | copy-start | bytes 388
  3.8 10.8 %copy-start.30 = (bf16[2,2,32,64]{3,2,1,0:T(8,128)(2,1)}, bf16[2,2,32,64]{3,2,1,0:T(8,128)(2,1)S(1)}, u32[]{:S(2)}) copy-start(bf16[2,2,32,64]{3,2,1,0:T(8,128)(2,1)S(1)} %fusion.129) | copy-start | bytes 49156
  4.0 94.9 %copy-start.14 = (f32[2,2,32,2,64]{4,2,3,1,0:T(8,128)}, f32[2,2,32,2,64]{4,2,3,1,0:T(8,128)S(1)}, u32[]{:S(2)}) copy-start(f32[2,2,32,2,64]{4,2,3,1,0:T(8,128)S(1)} %fusion.126) | copy-start | bytes 196612
  6.1 6.0 %copy-start.40 = (f32[32]{0:T(128)}, f32[32]{0:T(128)S(1)}, u32[]{:S(2)}) copy-start(f32[32]{0:T(128)S(1)} %add_rsqrt_fusion.2) | copy-start | bytes 388
  12.2 2.3 %copy-start.32 = (f32[2,2,32,2,8]{2,4,3,1,0:T(8,128)}, f32[2,2,32,2,8]{2,4,3,1,0:T(8,128)S(1)}, u32[]{:S(2)}) copy-start(f32[2,2,32,2,8]{2,4,3,1,0:T(8,128)S(1)} %fusion.152) | copy-start | bytes 24580
  13.8 38.2 %copy-start.38 = (f32[32,2]{0,1:T(2,128)}, f32[32,2]{0,1:T(2,128)S(1)}, u32[]{:S(2)}) copy-start(f32[32,2]{0,1:T(2,128)S(1)} %get-tuple-element.49) | copy-start | bytes 772
  14.6 1.0 copy-start.1
  48.5 1.0 copy-start.4
  49.7 2.3 %copy-start.5 = (bf16[32,8,2176]{2,1,0:T(8,128)(2,1)S(1)}, bf16[32,8,2176]{2,1,0:T(8,128)(2,1)}, u32[]{:S(2)}) copy-start(bf16[32,8,2176]{2,1,0:T(8,128)(2,1)} %copy-done.4) | copy-start | bytes 3342340
  49.7 2.3 %copy-start.8 = (bf16[1,256,2048]{2,1,0:T(8,128)(2,1)S(1)}, bf16[1,256,2048]{2,1,0:T(8,128)(2,1)}, u32[]{:S(2)}) copy-start(bf16[1,256,2048]{2,1,0:T(8,128)(2,1)} %param.24) | copy-start | bytes 3145732
  52.0 1.7 copy-start.17
  52.0 2.4 %copy-start.6 = (bf16[1,2048,256]{2,1,0:T(8,128)(2,1)S(1)}, bf16[1,2048,256]{2,1,0:T(8,128)(2,1)}, u32[]{:S(2)}) copy-start(bf16[1,2048,256]{2,1,0:T(8,128)(2,1)} %param.22) | copy-start | bytes 3145732
  58.2 1.9 %copy-start.18 = (f32[256,256]{1,0:T(8,128)S(1)}, f32[256,256]{1,0:T(8,128)}, u32[]{:S(2)}) copy-start(f32[256,256]{1,0:T(8,128)} %get-tuple-element.64) | copy-start | bytes 786436
  60.6 26.7 %copy-start.45 = (f32[32,2]{0,1:T(2,128)S(1)}, f32[32,2]{0,1:T(2,128)}, u32[]{:S(2)}) copy-start(f32[32,2]{0,1:T(2,128)} %get-tuple-element.55) | copy-start | bytes 772
  60.6 26.8 %copy-start.13 = (bf16[1,32,2048]{2,1,0:T(8,128)(2,1)S(1)}, bf16[1,32,2048]{2,1,0:T(8,128)(2,1)}, u32[]{:S(2)}) copy-start(bf16[1,32,2048]{2,1,0:T(8,128)(2,1)} %param.13) | copy-start | bytes 393220
  86.2 0.8 copy-start.2
  87.0 9.2 %copy-start.39 = (f32[32,2]{0,1:T(2,128)S(1)}, f32[32,2]{0,1:T(2,128)}, u32[]{:S(2)}) copy-start(f32[32,2]{0,1:T(2,128)} %copy-done.38) | copy-start | bytes 772
  87.0 9.3 %copy-start.34 = (bf16[1,32,2048]{2,1,0:T(8,128)(2,1)S(1)}, bf16[1,32,2048]{2,1,0:T(8,128)(2,1)}, u32[]{:S(2)}) copy-start(bf16[1,32,2048]{2,1,0:T(8,128)(2,1)} %param.14) | copy-start | bytes 393220
  87.0 8.7 %copy-start.3 = (bf16[16,8,2048]{2,1,0:T(8,128)(2,1)S(1)}, bf16[16,8,2048]{2,1,0:T(8,128)(2,1)}, u32[]{:S(2)}) copy-start(bf16[16,8,2048]{2,1,0:T(8,128)(2,1)} %copy-done.2) | copy-start | bytes 1572868
  87.0 9.4 %copy-start.29 = (f32[1,2048]{1,0:T(1,128)S(1)}, f32[1,2048]{1,0:T(1,128)}, u32[]{:S(2)}) copy-start(f32[1,2048]{1,0:T(1,128)} %param.20) | copy-start | bytes 24580
  87.0 9.4 %copy-start.35 = (bf16[1,2048,8]{1,2,0:T(8,128)(2,1)S(1)}, bf16[1,2048,8]{1,2,0:T(8,128)(2,1)}, u32[]{:S(2)}) copy-start(bf16[1,2048,8]{1,2,0:T(8,128)(2,1)} %param.21) | copy-start | bytes 98308
  87.1 9.6 %copy-start.33 = (f32[2,2,32,2,8]{2,4,3,1,0:T(8,128)S(1)}, f32[2,2,32,2,8]{2,4,3,1,0:T(8,128)}, u32[]{:S(2)}) copy-start(f32[2,2,32,2,8]{2,4,3,1,0:T(8,128)} %copy-done.32) | copy-start | bytes 24580
  87.2 9.6 %copy-start.9 = (bf16[2,1,32,2048]{3,2,1,0:T(8,128)(2,1)S(1)}, bf16[2,1,32,2048]{3,2,1,0:T(8,128)(2,1)}, u32[]{:S(2)}) copy-start(bf16[2,1,32,2048]{3,2,1,0:T(8,128)(2,1)} %param.15) | copy-start | bytes 786436
  87.8 8.9 %copy-start.23 = (bf16[32,2048]{1,0:T(8,128)(2,1)}, bf16[32,2048]{1,0:T(8,128)(2,1)S(1)}, u32[]{:S(2)}) copy-start(bf16[32,2048]{1,0:T(8,128)(2,1)S(1)} %fusion.12) | copy-start | bytes 393220
  87.8 11.8 %copy-start.20 = (bf16[1,32,2048]{2,1,0:T(8,128)(2,1)S(1)}, bf16[1,32,2048]{2,1,0:T(8,128)(2,1)}, u32[]{:S(2)}) copy-start(bf16[1,32,2048]{2,1,0:T(8,128)(2,1)} %param.16) | copy-start | bytes 393220
  87.8 11.8 %copy-start.41 = (f32[32]{0:T(128)S(1)}, f32[32]{0:T(128)}, u32[]{:S(2)}) copy-start(f32[32]{0:T(128)} %copy-done.40) | copy-start | bytes 388
  87.8 8.4 %collective-permute-start = (bf16[32,2048]{1,0:T(8,128)(2,1)S(1)}, bf16[32,2048]{1,0:T(8,128)(2,1)S(1)}, u32[]{:S(2)}, u32[]{:S(2)}) collective-permute-start(bf16[32,2048]{1,0:T(8,128)(2,1)S(1)} %fusion.12), channel_id=1, source_target_pairs={{0,32},{32,64},{64,96},{96,128},{128,160},{160,192},{192,224},{224... | collective-permute-start | bytes 393224 | tf_op jit(solution)/shard_map/ppermute | solution.py:18
  95.7 5.5 %copy-start.31 = (bf16[2,2,32,64]{3,2,1,0:T(8,128)(2,1)S(1)}, bf16[2,2,32,64]{3,2,1,0:T(8,128)(2,1)}, u32[]{:S(2)}) copy-start(bf16[2,2,32,64]{3,2,1,0:T(8,128)(2,1)} %copy-done.30) | copy-start | bytes 49156
  95.8 10.5 %copy-start.21 = (bf16[1,32,2048]{2,1,0:T(8,128)(2,1)S(1)}, bf16[1,32,2048]{2,1,0:T(8,128)(2,1)}, u32[]{:S(2)}) copy-start(bf16[1,32,2048]{2,1,0:T(8,128)(2,1)} %param.17) | copy-start | bytes 393220
  96.5 10.2 %copy-start.11 = (bf16[32,2048]{1,0:T(8,128)(2,1)}, bf16[32,2048]{1,0:T(8,128)(2,1)S(1)}, u32[]{:S(2)}) copy-start(bf16[32,2048]{1,0:T(8,128)(2,1)S(1)} %get-tuple-element.52) | copy-start | bytes 393220
  96.8 42.0 %copy-start.7 = (bf16[1,2048,256]{2,1,0:T(8,128)(2,1)S(1)}, bf16[1,2048,256]{2,1,0:T(8,128)(2,1)}, u32[]{:S(2)}) copy-start(bf16[1,2048,256]{2,1,0:T(8,128)(2,1)} %param.22) | copy-start | bytes 3145732
  98.0 8.6 %copy-start.42 = (f32[32]{0:T(128)}, f32[32]{0:T(128)S(1)}, u32[]{:S(2)}) copy-start(f32[32]{0:T(128)S(1)} %add_rsqrt_fusion) | copy-start | bytes 388
  99.8 6.8 %copy-start.25 = (bf16[32,2048]{1,0:T(8,128)(2,1)}, bf16[32,2048]{1,0:T(8,128)(2,1)S(1)}, u32[]{:S(2)}) copy-start(bf16[32,2048]{1,0:T(8,128)(2,1)S(1)} %fusion.87) | copy-start | bytes 393220
  99.8 5.9 %collective-permute-start.1 = (bf16[32,2048]{1,0:T(8,128)(2,1)S(1)}, bf16[32,2048]{1,0:T(8,128)(2,1)S(1)}, u32[]{:S(2)}, u32[]{:S(2)}) collective-permute-start(bf16[32,2048]{1,0:T(8,128)(2,1)S(1)} %fusion.87), channel_id=1, source_target_pairs={{32,0},{64,32},{96,64},{128,96},{160,128},{192,160},{224,192},{256... | collective-permute-start | bytes 393224 | tf_op jit(solution)/shard_map/ppermute | solution.py:18
  148.8 2.0 %copy-start.10 = (f32[256,256]{1,0:T(8,128)S(1)}, f32[256,256]{1,0:T(8,128)}, u32[]{:S(2)}) copy-start(f32[256,256]{1,0:T(8,128)} %fusion.17) | copy-start | bytes 786436
  148.8 2.0 %copy-start.16 = (f32[256,256]{1,0:T(8,128)S(1)}, f32[256,256]{1,0:T(8,128)}, u32[]{:S(2)}) copy-start(f32[256,256]{1,0:T(8,128)} %get-tuple-element.67) | copy-start | bytes 786436
  151.4 23.8 %copy-start.15 = (f32[2,2,32,2,64]{4,2,3,1,0:T(8,128)S(1)}, f32[2,2,32,2,64]{4,2,3,1,0:T(8,128)}, u32[]{:S(2)}) copy-start(f32[2,2,32,2,64]{4,2,3,1,0:T(8,128)} %copy-done.14) | copy-start | bytes 196612
  151.4 23.8 %copy-start.44 = (f32[32,2]{0,1:T(2,128)S(1)}, f32[32,2]{0,1:T(2,128)}, u32[]{:S(2)}) copy-start(f32[32,2]{0,1:T(2,128)} %get-tuple-element.53) | copy-start | bytes 772
  151.5 24.7 %copy-start.37 = (f32[32,64]{1,0:T(8,128)S(1)}, f32[32,64]{1,0:T(8,128)}, u32[]{:S(2)}) copy-start(f32[32,64]{1,0:T(8,128)} %get-tuple-element.43) | copy-start | bytes 24580
  175.0 1.6 copy-start.36
  175.0 1.6 copy-start.43
  175.0 2.0 %copy-start.12 = (bf16[32,2048]{1,0:T(8,128)(2,1)S(1)}, bf16[32,2048]{1,0:T(8,128)(2,1)}, u32[]{:S(2)}) copy-start(bf16[32,2048]{1,0:T(8,128)(2,1)} %copy-done.11) | copy-start | bytes 393220
  176.0 1.5 copy-start.22
  176.0 1.5 copy-start.28
  176.0 1.6 copy-start.26
  176.2 2.2 %copy-start.24 = (bf16[32,2048]{1,0:T(8,128)(2,1)S(1)}, bf16[32,2048]{1,0:T(8,128)(2,1)}, u32[]{:S(2)}) copy-start(bf16[32,2048]{1,0:T(8,128)(2,1)} %copy-done.23) | copy-start | bytes 393220
  (2 other events, 1.4 us)

commit v3 on v2

--- a/solution.py
+++ b/solution.py
@@ -42,6 +42,13 @@
         return (self.section, self.chip * 2 + 1 - self.core)
 
     def greet(self):
+        self.say()
+        self.heard()
+
+    def heard(self):
+        pl.semaphore_wait(pltpu.get_barrier_semaphore(), CHIPS)
+
+    def say(self):
         barrier = pltpu.get_barrier_semaphore()
 
         def signal(step, carry):
@@ -57,7 +64,6 @@
         pl.semaphore_signal(
             barrier, inc=1, device_id=self.other_core(), device_id_type=MESH
         )
-        pl.semaphore_wait(barrier, CHIPS)
 
 
 def steps_of(first, body):
@@ -140,13 +146,21 @@
     steps_of(0, finish)
 
 
-def collect_kernel(number, *refs):
-    parts, results = refs[:number], refs[number : 2 * number]
-    arrived, joined = refs[2 * number : 3 * number], refs[3 * number : 4 * number]
-    send, recv, pass_send, pass_recv = refs[4 * number :]
+def times(left, right, right_dim):
+    return lax.dot_general(
+        left, right, (((1,), (right_dim,)), ((), ())), preferred_element_type=jnp.float32
+    )
+
+
+def work_kernel(*refs):
+    rows_f, rows_b, carried, gate_ref, up_ref, down_ref = refs[:6]
+    results, parts, arrived, joined = refs[6:9], refs[9:12], refs[12:15], refs[15:18]
+    send, recv, pass_send, pass_recv = refs[18:]
+    sources, capacity, width = rows_f.shape
+    total_rows = sources * capacity
+    f32, bf16 = jnp.float32, jnp.bfloat16
     at = Place()
-    at.greet()
-    streams = range(number)
+    at.say()
 
     def passed(i, step):
         goal = at.away(step, 1)
@@ -171,38 +185,76 @@
     def added(i, step):
         passed(i, step).wait_recv()
         goal = at.away(step, 1)
-        total = parts[i][at.core * CHIPS + goal].astype(jnp.float32) + arrived[i][goal].astype(
-            jnp.float32
-        )
-        return goal, total.astype(jnp.bfloat16)
-
-    def start(step):
-        for i in streams:
-            passed(i, step).start()
-
-    def send_on(step):
-        for i in streams:
-            goal, total = added(i, step)
-            joined[i][goal] = total
-            outward(i, step).start()
+        total = parts[i][at.core * CHIPS + goal].astype(f32) + arrived[i][goal].astype(f32)
+        return goal, total.astype(bf16)
+
+    def send_all(streams):
+        def send_on(step):
+            for i in streams:
+                goal, total = added(i, step)
+                joined[i][goal] = total
+                outward(i, step).start()
+
+        steps_of(1, send_on)
+        for i in streams:
+            goal, total = added(i, 0)
+            results[i][goal] = total
+
+    def pass_all(streams):
+        def start(step):
+            for i in streams:
+                passed(i, step).start()
+
+        steps_of(1, start)
+        for i in streams:
+            passed(i, 0).start()
 
     def finish(step):
-        for i in streams:
+        for i in range(3):
             outward(i, step).wait_send()
             outward(i, step).wait_recv()
 
-    def sent(step):
-        for i in streams:
+    def handed(step):
+        for i in range(3):
             passed(i, step).wait_send()
 
-    steps_of(1, start)
-    for i in streams:
-        passed(i, 0).start()
-    steps_of(1, send_on)
-    for i in streams:
-        goal, total = added(i, 0)
-        results[i][goal] = total
-    steps_of(0, sent)
+    def flat(value):
+        return value.astype(f32).reshape(total_rows, value.shape[-1]).astype(bf16)
+
+    def first(rows):
+        value = flat(rows[...])
+        pre_gate = times(value, gate_ref[...], 0)
+        pre_up = times(value, up_ref[...], 0)
+        sigmoid_g = 1.0 / (1.0 + jnp.exp(-pre_gate))
+        activated = pre_gate * sigmoid_g
+        return pre_gate, pre_up, sigmoid_g, activated, (activated * pre_up).astype(bf16)
+
+    chunk = min(width, 512)
+
+    def store(i, at_col, value):
+        shape = (sources, capacity, value.shape[-1])
+        parts[i][:, :, at_col : at_col + value.shape[-1]] = value.reshape(shape).astype(bf16)
+
+    hidden_f = first(rows_f)[-1]
+    for col in range(0, width, chunk):
+        store(0, col, times(hidden_f, down_ref[:, col : col + chunk], 0))
+    at.heard()
+    pass_all([0])
+    pre_gate, pre_up, sigmoid_g, activated, hidden_b = first(rows_b)
+    plain_h = times(flat(carried[:, :, :width]), down_ref[...], 1)
+    send_all([0])
+    scales = carried[:, :, width:].astype(f32).reshape(total_rows, LANES)[:, :1]
+    inner_dot = jnp.sum(plain_h * hidden_b.astype(f32), axis=-1, keepdims=True)
+    back_h = plain_h * scales
+    d_gate = (back_h * pre_up * sigmoid_g * (1.0 + pre_gate * (1.0 - sigmoid_g))).astype(bf16)
+    d_up = (back_h * activated).astype(bf16)
+    for col in range(0, width, chunk):
+        part = times(d_gate, gate_ref[col : col + chunk, :], 1)
+        store(1, col, part + times(d_up, up_ref[col : col + chunk, :], 1))
+    store(2, 0, jnp.broadcast_to(inner_dot, (total_rows, LANES)))
+    pass_all([1, 2])
+    send_all([1, 2])
+    steps_of(0, handed)
     steps_of(1, finish)
 
 
@@ -223,57 +275,26 @@
     )(*arrays)
 
 
-def collect_rows(arrays):
-    number = len(arrays)
+def work_rows(rows_f, rows_b, carried, gate_q, up_q, down_q):
+    capacity, width = rows_f.shape[1:]
     whole = pl.BlockSpec(memory_space=pltpu.VMEM)
     sems = pltpu.SemaphoreType.DMA
-    blocks = [(CHIPS,) + a.shape[1:] for a in arrays]
+    tails = [(capacity, width), (capacity, width), (capacity, LANES)]
+
+    def spaces(lead):
+        return [pltpu.VMEM((lead,) + tail, jnp.bfloat16) for tail in tails]
+
     return pl.pallas_call(
-        functools.partial(collect_kernel, number),
-        out_shape=[jax.ShapeDtypeStruct(s, a.dtype) for s, a in zip(blocks, arrays)],
-        in_specs=[whole] * number,
-        out_specs=[whole] * number,
-        scratch_shapes=[pltpu.VMEM(s, a.dtype) for s, a in zip(blocks, arrays)] * 2
-        + [sems((number, CHIPS))] * 4,
+        work_kernel,
+        out_shape=[jax.ShapeDtypeStruct((CHIPS,) + tail, jnp.bfloat16) for tail in tails],
+        in_specs=[whole] * 6,
+        out_specs=[whole] * 3,
+        scratch_shapes=spaces(2 * CHIPS) + spaces(CHIPS) * 2 + [sems((3, CHIPS))] * 4,
         compiler_params=pltpu.CompilerParams(
-            collective_id=1, has_side_effects=True, vmem_limit_bytes=32 * 2**20
+            collective_id=1, has_side_effects=True, vmem_limit_bytes=40 * 2**20
         ),
-        name="collect_rows",
-    )(*arrays)
-
-
-def expert_work(rows_f, rows_b, carried, gate_q, up_q, down_q):
-    sources, capacity, width = rows_f.shape
-
-    def first(rows):
-        flat = rows.reshape(sources * capacity, width)
-        pre_gate = jnp.dot(flat, gate_q, preferred_element_type=jnp.float32)
-        pre_up = jnp.dot(flat, up_q, preferred_element_type=jnp.float32)
-        sigmoid_g = jax.nn.sigmoid(pre_gate)
-        activated = pre_gate * sigmoid_g
-        hidden = (activated * pre_up).astype(jnp.bfloat16)
-        return pre_gate, pre_up, sigmoid_g, activated, hidden
-
-    hidden_f = first(rows_f)[-1]
-    pre_gate, pre_up, sigmoid_g, activated, hidden_b = first(rows_b)
-    y_part = jnp.dot(hidden_f, down_q, preferred_element_type=jnp.float32).astype(jnp.bfloat16)
-    grads = carried[:, :, :width].reshape(sources * capacity, width)
-    scales = carried[:, :, width].reshape(sources * capacity, 1).astype(jnp.float32)
-    plain_h = jnp.dot(grads, down_q.T, preferred_element_type=jnp.float32)
-    inner_dot = jnp.sum(plain_h * hidden_b.astype(jnp.float32), axis=-1, keepdims=True)
-    back_h = plain_h * scales
-    d_gate = back_h * pre_up * sigmoid_g * (1.0 + pre_gate * (1.0 - sigmoid_g))
-    d_up = back_h * activated
-    dn_part = jnp.dot(
-        d_gate.astype(jnp.bfloat16), gate_q.T, preferred_element_type=jnp.float32
-    ) + jnp.dot(d_up.astype(jnp.bfloat16), up_q.T, preferred_element_type=jnp.float32)
-    dots = jnp.broadcast_to(inner_dot, (sources * capacity, LANES)).astype(jnp.bfloat16)
-    shape = (sources, capacity)
-    return (
-        y_part.reshape(shape + (width,)),
-        dn_part.astype(jnp.bfloat16).reshape(shape + (width,)),
-        dots.reshape(shape + (LANES,)),
-    )
+        name="work_rows",
+    )(rows_f, rows_b, carried, gate_q, up_q, down_q)
 
 
 def on_device(
@@ -376,10 +397,10 @@
         if totals is None:
             seen = got_carried[:, 0, width + 1 : width + 1 + TICKS].astype(f32)
             totals = jnp.sum(seen, axis=0)
-        partial = expert_work(got_f, got_b, got_carried, gate_cols, up_cols, down_rows)
+        outputs = work_rows(got_f, got_b, got_carried, gate_cols, up_cols, down_rows)
         halves = [
             jnp.sum(part.astype(f32).reshape(experts, 2, capacity, -1), axis=1).reshape(slots, -1)
-            for part in collect_rows(partial)
+            for part in outputs
         ]
         y_sum, dn_sum, dot_sum = halves
         combine_f = jnp.sum(table[0, k] * gate_f[:, :, None], axis=1)

time: 183 us -> 156 us (0.85)
  matrix products: 32.3 us -> 10.4 us
  Pallas kernels: 114 us -> 108 us
  other arithmetic: 12.8 us -> 16.1 us
  local copies, waits for them, and re-layouts: 7.36 us -> 5.39 us
    dot_general x14 -> x0, matrix products: 22.4 us -> none  [the longest x4 6.47 us: first(): pre_gate = jnp.dot(flat, gate_q, preferred_element_type=jnp.float32)]
    pallas_call x2, Pallas kernels: 49 us -> 44.9 us  [work_rows(): pl.pallas_call(work_kernel, out_shape=[jax.ShapeDtypeStruct((CHIPS,) + ta...]
    pallas_call x2, Pallas kernels: 64.9 us -> 62.9 us  [dispatch_rows(): pl.pallas_call(functools.partial(dispatch_kernel, number), out_shape=[jax...]
    reduce_sum x5, other arithmetic: 0.35 us -> 2.28 us  [on_device(): jnp.sum(part.astype(f32).reshape(experts, 2, capacity, -1), axis=1)]
    unnamed x97 -> x43, local copies, waits for them, and re-layouts: 4.37 us -> 3.57 us
  transfers between devices with their start and end apart: 2 -> 2, of which waited for: 1 -> 1; matrix products, arithmetic and copies ran while one was open for 2% -> 3% of each run, Pallas kernels for 0% -> 0%
where the time goes in v3:
time: 156 us; the launch traced here: 154 us
  Pallas kernels  108 us (69%)
  other arithmetic  16.1 us (10%)
  matrix products  10.4 us (7%)
  starting transfers between devices  6.14 us (4%)
  local copies, waits for them, and re-layouts  5.39 us (3%)
  between operations  4.35 us (3%)
  waiting for transfers between devices  3.68 us (2%)
    pallas_call x2, Pallas kernels, dispatch_rows(): pl.pallas_call(functools.partial(dispatch_kernel, number), out_shape=[jax...  62.9 us
    pallas_call x2, Pallas kernels, work_rows(): pl.pallas_call(work_kernel, out_shape=[jax.ShapeDtypeStruct((CHIPS,) + ta...  44.9 us
    ppermute x2, starting transfers between devices, from_behind(): return lax.ppermute(block, axis, route)  6.14 us
    ppermute x2, waiting for transfers between devices, from_behind(): return lax.ppermute(block, axis, route)  3.68 us
    unnamed x43, local copies, waits for them, and re-layouts  3.57 us
    dot_general x6, matrix products, placed(): lax.dot_general(dispatch[m, k], rows, (((0,), (0,)), ((), ())), preferred...  3.2 us
    reduce_sum x3, other arithmetic, norm_of(): jnp.mean(values * values, axis=-1, keepdims=True) + 1e-05  3.15 us
  transfers between devices with their start and end apart: 2, of which 1 were waited for; matrix products, arithmetic and copies ran while one was open for 3% of the time, Pallas kernels for 0%

profile of v3, /device:TPU:1, one launch (start us, length us, event | category | flops | bytes accessed | tf_op | source)
XLA Modules:
  0.0 153.9 jit_solution(3709330956008263777)
XLA Ops:
  0.7 0.5 iota_compare_fusion.4
  1.2 0.8 slice_reduce_fusion.4
  2.0 0.7 fusion.91
  2.7 0.8 copy.61
  3.6 0.2 convert_reduce_fusion.4
  4.1 0.1 fusion.53
  4.2 0.8 fusion.52
  5.0 1.0 fusion.40
  6.1 1.0 fusion.34
  7.2 1.8 %fusion.73 = f32[32,8]{0,1:T(8,128)} fusion(bf16[1,2048,8]{1,2,0:T(8,128)(2,1)S(1)} %copy-done, f32[2048]{0:T(1024)} %bitcast.270, f32[32]{0:T(128)S(1)} %add_rsqrt_fusion.2, bf16[2,1,32,2048]{3,2,1,0:T(8,128)(2,1)} %param.15), kind=kOutput, calls=%fused_computation.110 | convolution fusion | flops 1310720 | bytes 173184 | tf_op jit(solution)/shard_map/dot_general | solution.py:352
  9.0 0.8 fusion.55
  9.8 0.3 fusion.refs_0_
  10.1 1.0 fusion.1.refs_1_
  11.1 0.6 fusion.93
  11.8 1.2 convolution_convert_fusion.3
  13.0 1.3 compare_select_fusion.5
  14.3 0.7 multiply_reduce_fusion.3
  15.0 0.9 fusion.66
  15.9 0.7 select_convert_fusion.1
  16.6 0.9 copy-done.4
  17.6 32.9 %dispatch_rows.2 = (bf16[32,8,2048]{2,1,0:T(8,128)(2,1)S(1)}, bf16[32,8,2048]{2,1,0:T(8,128)(2,1)S(1)}, bf16[32,8,2176]{2,1,0:T(8,128)(2,1)S(1)}) custom-call(bf16[8,8,2048]{2,1,0:T(8,128)(2,1)S(1)} %fusion.refs_0_, bf16[8,8,2048]{2,1,0:T(8,128)(2,1)S(1)} %copy-done.4, bf16[8,8,2176]{2,1,0:T(8,128)(2,1)S(1)} %maximum_bitcast_fusion.refs_2_), custom_call_target="tpu_custom_call" | custom-call | tf_op jit(solution)/shard_map/dispatch_rows/pallas_call | solution.py:265
  50.5 22.8 %work_rows.2 = (bf16[16,8,2048]{2,1,0:T(8,128)(2,1)S(1)}, bf16[16,8,2048]{2,1,0:T(8,128)(2,1)S(1)}, bf16[16,8,128]{2,1,0:T(8,128)(2,1)S(1)}) custom-call(bf16[32,8,2048]{2,1,0:T(8,128)(2,1)S(1)} %get-tuple-element.15.refs_0_, bf16[32,8,2048]{2,1,0:T(8,128)(2,1)S(1)} %get-tuple-element.16.refs_1_, bf16[32,8,2176]{2,1,0:T(8,128)(2,1)S(1)} %get-tuple-element.17.refs_2_, ...), custom_call_target="tpu_custom_call" | custom-call | tf_op jit(solution)/shard_map/work_rows/pallas_call | solution.py:287
  73.3 0.8 copy-done.5
  74.3 0.7 copy-done.10
  75.1 1.0 fusion.6
  76.2 4.7 %collective-permute-start = (bf16[32,2048]{1,0:T(8,128)(2,1)}, bf16[32,2048]{1,0:T(8,128)(2,1)}, u32[]{:S(2)}, u32[]{:S(2)}) collective-permute-start(bf16[32,2048]{1,0:T(8,128)(2,1)} %fusion.6), channel_id=1, source_target_pairs={{0,32},{32,64},{64,96},{96,128},{128,160},{160,192},{192,224},{224... | collective-permute-start | bytes 393224 | tf_op jit(solution)/shard_map/ppermute | solution.py:18
  80.8 0.6 slice_reduce_fusion.2
  82.2 0.6 fusion.92
  84.3 2.0 %convert_reduce_fusion.2 = f32[8,8,2048]{2,1,0:T(8,128)} fusion(bf16[16,8,2048]{2,1,0:T(8,128)(2,1)} %copy-done.5), kind=kLoop, calls=%fused_computation.21 | loop fusion | flops 393216 | bytes 1048576 | tf_op jit(solution)/shard_map/reduce_sum | solution.py:402
  86.3 1.5 fusion.12
  87.8 1.1 fusion.43
  88.9 0.2 fusion.58
  89.1 0.4 fusion.29
  89.6 0.2 fusion.69
  90.2 1.5 collective-permute-start.1
  91.7 0.3 fusion.2.refs_0_
  92.0 0.3 fusion.3.refs_1_
  92.2 3.7 %collective-permute-done.1 = bf16[32,2048]{1,0:T(8,128)(2,1)S(1)} collective-permute-done((bf16[32,2048]{1,0:T(8,128)(2,1)S(1)}, bf16[32,2048]{1,0:T(8,128)(2,1)S(1)}, u32[]{:S(2)}, u32[]{:S(2)}) %collective-permute-start.1) | collective-permute-done | bytes 131104 | tf_op jit(solution)/shard_map/ppermute | solution.py:18
  95.9 0.2 convolution_convert_fusion
  96.2 30.0 %dispatch_rows.3 = (bf16[32,8,2048]{2,1,0:T(8,128)(2,1)S(1)}, bf16[32,8,2048]{2,1,0:T(8,128)(2,1)S(1)}, bf16[32,8,2176]{2,1,0:T(8,128)(2,1)S(1)}) custom-call(bf16[8,8,2048]{2,1,0:T(8,128)(2,1)S(1)} %fusion.2.refs_0_, bf16[8,8,2048]{2,1,0:T(8,128)(2,1)S(1)} %fusion.3.refs_1_, bf16[8,8,2176]{2,1,0:T(8,128)(2,1)S(1)} %maximum_bitcast_fusion.1.refs_2_), custom_call_target="tpu_custom_call" | custom-call | tf_op jit(solution)/shard_map/dispatch_rows/pallas_call | solution.py:265
  126.3 22.1 %work_rows.3 = (bf16[16,8,2048]{2,1,0:T(8,128)(2,1)S(1)}, bf16[16,8,2048]{2,1,0:T(8,128)(2,1)S(1)}, bf16[16,8,128]{2,1,0:T(8,128)(2,1)S(1)}) custom-call(bf16[32,8,2048]{2,1,0:T(8,128)(2,1)S(1)} %get-tuple-element.21.refs_0_, bf16[32,8,2048]{2,1,0:T(8,128)(2,1)S(1)} %get-tuple-element.22.refs_1_, bf16[32,8,2176]{2,1,0:T(8,128)(2,1)S(1)} %get-tuple-element.23.refs_2_, ...), custom_call_target="tpu_custom_call" | custom-call | tf_op jit(solution)/shard_map/work_rows/pallas_call | solution.py:287
  148.6 0.2 convert_reduce_fusion
  148.8 0.3 copy-done.15
  149.1 0.4 fusion.9
  149.4 0.4 fusion.24
  149.9 0.4 fusion.8
  150.4 0.7 maximum_bitcast_fusion.3
  151.1 1.6 %maximum_bitcast_fusion.2 = bf16[2,1,32,2048]{3,2,1,0:T(8,128)(2,1)} fusion(bf16[1,32,2048]{2,1,0:T(8,128)(2,1)S(1)} %fusion.8, bf16[1,32,2048]{2,1,0:T(8,128)(2,1)} %bitcast.27), kind=kLoop, calls=%fused_computation.70 | loop fusion | flops 131072 | bytes 524288
  (74 shorter events, 1.8 us)
Async XLA Ops:
  0.6 6.5 %copy-start = (bf16[1,2048,8]{1,2,0:T(8,128)(2,1)S(1)}, bf16[1,2048,8]{1,2,0:T(8,128)(2,1)}, u32[]{:S(2)}) copy-start(bf16[1,2048,8]{1,2,0:T(8,128)(2,1)} %param.21) | copy-start | bytes 98308
  0.6 8.4 %copy-start.8 = (bf16[1,32,2048]{2,1,0:T(8,128)(2,1)S(1)}, bf16[1,32,2048]{2,1,0:T(8,128)(2,1)}, u32[]{:S(2)}) copy-start(bf16[1,32,2048]{2,1,0:T(8,128)(2,1)} %param.13) | copy-start | bytes 393220
  0.7 8.3 %copy-start.14 = (f32[1,2048]{1,0:T(1,128)S(1)}, f32[1,2048]{1,0:T(1,128)}, u32[]{:S(2)}) copy-start(f32[1,2048]{1,0:T(1,128)} %param.20) | copy-start | bytes 24580
  4.1 6.0 %copy-start.6 = (bf16[2,1,32,2048]{3,2,1,0:T(8,128)(2,1)S(1)}, bf16[2,1,32,2048]{3,2,1,0:T(8,128)(2,1)}, u32[]{:S(2)}) copy-start(bf16[2,1,32,2048]{3,2,1,0:T(8,128)(2,1)} %param.15) | copy-start | bytes 786436
  7.1 4.6 %copy-start.16 = (f32[32]{0:T(128)}, f32[32]{0:T(128)S(1)}, u32[]{:S(2)}) copy-start(f32[32]{0:T(128)S(1)} %add_rsqrt_fusion.2) | copy-start | bytes 388
  7.2 43.3 %copy-start.3 = (bf16[1,256,2048]{2,1,0:T(8,128)(2,1)S(1)}, bf16[1,256,2048]{2,1,0:T(8,128)(2,1)}, u32[]{:S(2)}) copy-start(bf16[1,256,2048]{2,1,0:T(8,128)(2,1)} %param.24) | copy-start | bytes 3145732
  10.1 40.3 %copy-start.1 = (bf16[1,2048,256]{2,1,0:T(8,128)(2,1)S(1)}, bf16[1,2048,256]{2,1,0:T(8,128)(2,1)}, u32[]{:S(2)}) copy-start(bf16[1,2048,256]{2,1,0:T(8,128)(2,1)} %param.22) | copy-start | bytes 3145732
  10.1 40.3 %copy-start.2 = (bf16[1,2048,256]{2,1,0:T(8,128)(2,1)S(1)}, bf16[1,2048,256]{2,1,0:T(8,128)(2,1)}, u32[]{:S(2)}) copy-start(bf16[1,2048,256]{2,1,0:T(8,128)(2,1)} %param.23) | copy-start | bytes 3145732
  14.3 59.0 %copy-start.19 = (bf16[128]{0:T(256)(128)(2,1)}, bf16[128]{0:T(256)(128)(2,1)S(1)}, u32[]{:S(2)}) copy-start(bf16[128]{0:T(256)(128)(2,1)S(1)} %compare_select_fusion.5) | copy-start | bytes 772
  16.6 1.0 copy-start.4
  73.3 0.8 copy-start.5
  74.1 0.9 copy-start.10
  74.1 1.0 copy-start.9
  76.2 11.6 %collective-permute-start = (bf16[32,2048]{1,0:T(8,128)(2,1)}, bf16[32,2048]{1,0:T(8,128)(2,1)}, u32[]{:S(2)}, u32[]{:S(2)}) collective-permute-start(bf16[32,2048]{1,0:T(8,128)(2,1)} %fusion.6), channel_id=1, source_target_pairs={{0,32},{32,64},{64,96},{96,128},{128,160},{160,192},{192,224},{224... | collective-permute-start | bytes 393224 | tf_op jit(solution)/shard_map/ppermute | solution.py:18
  84.2 4.9 %copy-start.7 = (bf16[2,1,32,2048]{3,2,1,0:T(8,128)(2,1)S(1)}, bf16[2,1,32,2048]{3,2,1,0:T(8,128)(2,1)}, u32[]{:S(2)}) copy-start(bf16[2,1,32,2048]{3,2,1,0:T(8,128)(2,1)} %param.15) | copy-start | bytes 786436
  84.2 4.9 %copy-start.17 = (f32[32]{0:T(128)S(1)}, f32[32]{0:T(128)}, u32[]{:S(2)}) copy-start(f32[32]{0:T(128)} %copy-done.16) | copy-start | bytes 388
  86.3 3.6 %copy-start.11 = (f32[2,2,32,2,64]{4,2,3,1,0:T(8,128)S(1)}, f32[2,2,32,2,64]{4,2,3,1,0:T(8,128)}, u32[]{:S(2)}) copy-start(f32[2,2,32,2,64]{4,2,3,1,0:T(8,128)} %fusion.52) | copy-start | bytes 196612
  86.3 3.7 %copy-start.18 = (pred[128]{0:T(512)(128)(4,1)S(1)}, pred[128]{0:T(512)(128)(4,1)}, u32[]{:S(2)}) copy-start(pred[128]{0:T(512)(128)(4,1)} %iota_compare_fusion.4) | copy-start | bytes 388
  86.3 3.7 %copy-start.20 = (bf16[128]{0:T(256)(128)(2,1)S(1)}, bf16[128]{0:T(256)(128)(2,1)}, u32[]{:S(2)}) copy-start(bf16[128]{0:T(256)(128)(2,1)} %copy-done.19) | copy-start | bytes 772
  86.3 3.8 %copy-start.12 = (bf16[1,32,2048]{2,1,0:T(8,128)(2,1)S(1)}, bf16[1,32,2048]{2,1,0:T(8,128)(2,1)}, u32[]{:S(2)}) copy-start(bf16[1,32,2048]{2,1,0:T(8,128)(2,1)} %param.16) | copy-start | bytes 393220
  89.6 6.4 %copy-start.13 = (bf16[1,32,2048]{2,1,0:T(8,128)(2,1)S(1)}, bf16[1,32,2048]{2,1,0:T(8,128)(2,1)}, u32[]{:S(2)}) copy-start(bf16[1,32,2048]{2,1,0:T(8,128)(2,1)} %param.17) | copy-start | bytes 393220
  90.2 5.7 %collective-permute-start.1 = (bf16[32,2048]{1,0:T(8,128)(2,1)S(1)}, bf16[32,2048]{1,0:T(8,128)(2,1)S(1)}, u32[]{:S(2)}, u32[]{:S(2)}) collective-permute-start(bf16[32,2048]{1,0:T(8,128)(2,1)S(1)} %fusion.33), channel_id=1, source_target_pairs={{32,0},{64,32},{96,64},{128,96},{160,128},{192,160},{224,192},{256... | collective-permute-start | bytes 393224 | tf_op jit(solution)/shard_map/ppermute | solution.py:18
  148.3 0.7 copy-start.15

commit v4 on v3

--- a/solution.py
+++ b/solution.py
@@ -85,12 +85,20 @@
     )
 
 
-def dispatch_kernel(number, *refs):
-    sources, results = refs[:number], refs[number : 2 * number]
-    send, recv, pass_send, pass_recv, own = refs[2 * number :]
+def dispatch_kernel(*refs):
+    move_f, move_b, given_f, given_b, given_g, extra = refs[:6]
+    results, sources = refs[6:9], refs[9:12]
+    send, recv, pass_send, pass_recv, own = refs[12:]
     at = Place()
-    at.greet()
-    streams = range(number)
+    at.say()
+    streams = range(3)
+    experts, capacity, width = sources[0].shape
+    for i, move, given in ((0, move_f, given_f), (1, move_b, given_b), (2, move_b, given_g)):
+        placed = times(move[...], given[...], 0).reshape(experts, capacity, width)
+        sources[i][:, :, :width] = placed.astype(jnp.bfloat16)
+    tail = extra[...].reshape(experts, capacity, LANES)
+    sources[2][:, :, width:] = tail.astype(jnp.bfloat16)
+    at.heard()
 
     def outward(i, step):
         goal = at.away(step, 1)
@@ -258,21 +266,25 @@
     steps_of(1, finish)
 
 
-def dispatch_rows(arrays):
-    number = len(arrays)
+def dispatch_rows(move_f, move_b, given_f, given_b, given_g, extra, experts):
+    width = given_f.shape[1]
+    capacity = move_f.shape[0] // experts
     whole = pl.BlockSpec(memory_space=pltpu.VMEM)
     sems = pltpu.SemaphoreType.DMA
+    tails = [(capacity, width), (capacity, width), (capacity, width + LANES)]
     return pl.pallas_call(
-        functools.partial(dispatch_kernel, number),
-        out_shape=[jax.ShapeDtypeStruct((2 * CHIPS,) + a.shape[1:], a.dtype) for a in arrays],
-        in_specs=[whole] * number,
-        out_specs=[whole] * number,
-        scratch_shapes=[sems((number, CHIPS))] * 4 + [sems((number,))],
+        dispatch_kernel,
+        out_shape=[jax.ShapeDtypeStruct((2 * CHIPS,) + t, jnp.bfloat16) for t in tails],
+        in_specs=[whole] * 6,
+        out_specs=[whole] * 3,
+        scratch_shapes=[pltpu.VMEM((experts,) + t, jnp.bfloat16) for t in tails]
+        + [sems((3, CHIPS))] * 4
+        + [sems((3,))],
         compiler_params=pltpu.CompilerParams(
             collective_id=0, has_side_effects=True, vmem_limit_bytes=32 * 2**20
         ),
         name="dispatch_rows",
-    )(*arrays)
+    )(move_f, move_b, given_f, given_b, given_g, extra)
 
 
 def work_rows(rows_f, rows_b, carried, gate_q, up_q, down_q):
@@ -339,7 +351,8 @@
     live = jnp.arange(top_slots, dtype=jnp.int32) < count[..., None]
     table = ((target[..., None] == jnp.arange(slots)) & live[..., None]).astype(f32)
     chosen = (route[..., None] == jnp.arange(experts)).astype(f32)
-    dispatch = jnp.sum(table, axis=3).astype(bf16)
+    held = (target[:, :, None] == jnp.arange(slots)[:, None, None]) & live[:, :, None]
+    moves = jnp.sum(held.astype(f32), axis=-1).astype(bf16)
     live = live.astype(f32)
     own_totals = jnp.sum(count[0], axis=-1).astype(f32)
 
@@ -351,11 +364,6 @@
     def picked_of(normed, m, k):
         logits = jnp.dot(normed, router, preferred_element_type=f32)
         return jnp.sum(chosen[m, k] * logits[:, None, :], axis=-1)
-
-    def placed(m, k, rows):
-        return lax.dot_general(
-            dispatch[m, k], rows, (((0,), (0,)), ((), ())), preferred_element_type=f32
-        ).astype(bf16)
 
     backs = []
     for k in range(TICKS):
@@ -364,7 +372,7 @@
         picked = picked_of(normed, 1, k)
         gate = jax.nn.softplus(picked) * live[1, k]
         scale = jnp.sum(table[1, k] * gate[:, :, None], axis=(0, 1))
-        backs.append((unit, inverse, placed(1, k, normed), picked, scale))
+        backs.append((unit, inverse, normed, picked, scale))
 
     weight = lam[0]
     forward_x = section_in[0]
@@ -378,7 +386,7 @@
             forward_x = jnp.where(section_pos == 0, new_batch[k - 1], arriving)
             coming = from_behind(grad_list[-1], "section", -1)
             cotangent = jnp.where(section_pos == last_section, loss_grad[k - 1], coming)
-        unit_b, inverse_b, rows_b, picked_b, scale_b = backs[k]
+        unit_b, inverse_b, normed_b, picked_b, scale_b = backs[k]
         unit_f, _ = norm_of(forward_x)
         normed_f = (unit_f * gain_row).astype(bf16)
         gate_f = jax.nn.softplus(picked_of(normed_f, 0, k)) * live[0, k]
@@ -387,12 +395,9 @@
             lane == 0,
             scale_b[:, None],
             jnp.where(lane == 1, own_totals[0], jnp.where(lane == 2, own_totals[1], 0.0)),
-        ).astype(bf16)
-        carried = jnp.concatenate([placed(1, k, cotangent), extra], axis=1)
-        carried = carried.reshape(experts, capacity, width + LANES)
-        grouped = (experts, capacity, width)
+        )
         got_f, got_b, got_carried = dispatch_rows(
-            [placed(0, k, normed_f).reshape(grouped), rows_b.reshape(grouped), carried]
+            moves[0, k], moves[1, k], normed_f, normed_b, cotangent, extra, experts
         )
         if totals is None:
             seen = got_carried[:, 0, width + 1 : width + 1 + TICKS].astype(f32)

time: 156 us -> 159 us (1.019)
  local copies, waits for them, and re-layouts: 5.39 us -> 9.69 us
  matrix products: 10.4 us -> 7.55 us
    dot_general x6 -> x0, matrix products: 3.2 us -> none  [placed(): lax.dot_general(dispatch[m, k], rows, (((0,), (0,)), ((), ())), preferred...]
    reduce_sum x1 -> x3, local copies, waits for them, and re-layouts: 0.12 us -> 2.4 us  [on_device(): jnp.sum(((flat[..., :, None] == flat[..., None, :]) & earlier).astype(jnp...]
    reduce_sum x5 -> x6, other arithmetic: 2.28 us -> 0.34 us  [on_device(): jnp.sum(part.astype(f32).reshape(experts, 2, capacity, -1), axis=1)]
    unnamed x43 -> x49, local copies, waits for them, and re-layouts: 3.57 us -> 3.16 us
  transfers between devices with their start and end apart: 2 -> 2, of which waited for: 1 -> 1; matrix products, arithmetic and copies ran while one was open for 3% -> 1% of each run, Pallas kernels for 0% -> 0%
where the time goes in v4:
time: 159 us; the launch traced here: 156 us
  Pallas kernels  108 us (68%)
  other arithmetic  16.8 us (11%)
  local copies, waits for them, and re-layouts  9.69 us (6%)
  matrix products  7.55 us (5%)
  starting transfers between devices  6.31 us (4%)
  between operations  4.27 us (3%)
  waiting for transfers between devices  4.22 us (3%)
    pallas_call x2, Pallas kernels, dispatch_rows(): pl.pallas_call(dispatch_kernel, out_shape=[jax.ShapeDtypeStruct((2 * CHIP...  62.9 us
    pallas_call x2, Pallas kernels, work_rows(): pl.pallas_call(work_kernel, out_shape=[jax.ShapeDtypeStruct((CHIPS,) + ta...  44.8 us
    ppermute x2, starting transfers between devices, from_behind(): return lax.ppermute(block, axis, route)  6.31 us
    ppermute x2, waiting for transfers between devices, from_behind(): return lax.ppermute(block, axis, route)  4.22 us
    dot_general x4, matrix products, picked_of(): logits = jnp.dot(normed, router, preferred_element_type=f32)  3.9 us
  transfers between devices with their start and end apart: 2, of which 1 were waited for; matrix products, arithmetic and copies ran while one was open for 1% of the time, Pallas kernels for 0%

profile of v4, /device:TPU:1, one launch (start us, length us, event | category | flops | bytes accessed | tf_op | source)
XLA Modules:
  0.0 156.5 jit_solution(2211539968339379359)
XLA Ops:
  0.7 0.6 iota_compare_fusion.5
  1.3 0.8 copy.79
  2.2 0.2 convert_reduce_fusion.5
  2.4 0.7 reduce_sum.279
  3.1 0.7 reduce_sum.275
  3.9 1.0 fusion.23
  4.9 1.0 fusion.34
  6.0 1.7 %fusion.57 = f32[32,8]{0,1:T(8,128)} fusion(bf16[1,32,2048]{2,1,0:T(8,128)(2,1)} %param.13, f32[2048]{0:T(1024)} %bitcast.263, f32[32]{0:T(128)S(1)} %get-tuple-element.75, bf16[1,2048,8]{1,2,0:T(8,128)(2,1)S(1)} %copy-done), kind=kOutput, calls=%fused_computation.73 | convolution fusion | flops 1310720 | bytes 173184 | tf_op jit(solution)/shard_map/dot_general | solution.py:365
  7.7 1.8 %fusion.54 = f32[32,8]{0,1:T(8,128)} fusion(f32[2048]{0:T(1024)} %bitcast.264, f32[32]{0:T(128)S(1)} %get-tuple-element.74, bf16[2,1,32,2048]{3,2,1,0:T(8,128)(2,1)} %param.15, bf16[1,2048,8]{1,2,0:T(8,128)(2,1)S(1)} %copy-done), kind=kOutput, calls=%fused_computation.71 | convolution fusion | flops 1310720 | bytes 173184 | tf_op jit(solution)/shard_map/dot_general | solution.py:365
  9.5 1.2 fusion.28
  11.5 0.7 fusion.98
  12.3 0.6 fusion.85
  12.9 0.9 copy.83
  14.0 0.7 copy.84
  14.7 0.8 slice_bitcast_fusion.4
  15.5 1.5 multiply_add_fusion
  17.0 0.9 copy.81
  17.9 0.1 fusion.66
  18.1 0.6 slice_reduce_fusion.2
  18.7 0.7 multiply_reduce_fusion.3
  19.5 1.3 compare_select_fusion.5
  20.8 0.7 broadcast_select_fusion.1.refs_5_
  21.6 0.9 copy-done.4
  22.5 32.9 %dispatch_rows.2 = (bf16[32,8,2048]{2,1,0:T(8,128)(2,1)S(1)}, bf16[32,8,2048]{2,1,0:T(8,128)(2,1)S(1)}, bf16[32,8,2176]{2,1,0:T(8,128)(2,1)S(1)}) custom-call(bf16[64,32]{1,0:T(8,128)(2,1)S(1)} %get-tuple-element.58.refs_0_, bf16[64,32]{1,0:T(8,128)(2,1)S(1)} %get-tuple-element.56.refs_1_, bf16[32,2048]{1,0:T(8,128)(2,1)S(1)} %get-tuple-element.62.refs_2_, ...), custom_call_target="tpu_custom_call" | custom-call | tf_op jit(solution)/shard_map/dispatch_rows/pallas_call | solution.py:275
  55.4 22.7 %work_rows.2 = (bf16[16,8,2048]{2,1,0:T(8,128)(2,1)S(1)}, bf16[16,8,2048]{2,1,0:T(8,128)(2,1)S(1)}, bf16[16,8,128]{2,1,0:T(8,128)(2,1)S(1)}) custom-call(bf16[32,8,2048]{2,1,0:T(8,128)(2,1)S(1)} %get-tuple-element.15.refs_0_, bf16[32,8,2048]{2,1,0:T(8,128)(2,1)S(1)} %get-tuple-element.16.refs_1_, bf16[32,8,2176]{2,1,0:T(8,128)(2,1)S(1)} %get-tuple-element.17.refs_2_, ...), custom_call_target="tpu_custom_call" | custom-call | tf_op jit(solution)/shard_map/work_rows/pallas_call | solution.py:299
  78.4 0.4 copy-done.12
  78.9 0.4 fusion.8
  79.4 1.7 %fusion.29 = (f32[32]{0:T(128)}, f32[32]{0:T(128)S(1)}, f32[32,2048]{1,0:T(8,128)}) fusion(f32[32]{0:T(128)S(1)} %copy-done.18, bf16[2,1,32,2048]{3,2,1,0:T(8,128)(2,1)S(1)} %copy-done.6, f32[2048]{0:T(1024)S(1)} %bitcast.266, f32[32,2048]{1,0:T(8,128)S(1)} %fusion.8, f32[32,8]{0,1:T(8,128)S(1)} %multiply_reduce_fusion.2, bf16[1,2048,8]{1,2,0:T(8,128)(2,1)S(1)} %copy-done), kind=kOutput, calls=%fused_computation.45 | convolution fusion | flops 6881216 | bytes 828800 | tf_op jit(solution)/shard_map/dot_general | solution.py:422
  81.0 0.2 fusion.50
  81.3 0.3 copy-done.19
  81.6 0.6 fusion.74
  82.2 0.4 fusion.2
  82.6 4.8 %collective-permute-start = (bf16[32,2048]{1,0:T(8,128)(2,1)S(1)}, bf16[32,2048]{1,0:T(8,128)(2,1)}, u32[]{:S(2)}, u32[]{:S(2)}) collective-permute-start(bf16[32,2048]{1,0:T(8,128)(2,1)S(1)} %fusion.2), channel_id=1, source_target_pairs={{0,32},{32,64},{64,96},{96,128},{128,160},{160,192},{192,224},{224... | collective-permute-start | bytes 393224 | tf_op jit(solution)/shard_map/ppermute | solution.py:18
  87.6 0.6 fusion.97
  89.6 0.7 broadcast_select_fusion.refs_5_
  90.3 0.7 broadcast_multiply_fusion.1
  91.0 1.1 fusion.46
  92.1 1.2 fusion.33
  93.5 1.5 collective-permute-start.1
  95.0 4.2 %collective-permute-done.1 = bf16[32,2048]{1,0:T(8,128)(2,1)S(1)} collective-permute-done((bf16[32,2048]{1,0:T(8,128)(2,1)S(1)}, bf16[32,2048]{1,0:T(8,128)(2,1)S(1)}, u32[]{:S(2)}, u32[]{:S(2)}) %collective-permute-start.1) | collective-permute-done | bytes 131104 | tf_op jit(solution)/shard_map/ppermute | solution.py:18
  99.2 30.0 %dispatch_rows.3 = (bf16[32,8,2048]{2,1,0:T(8,128)(2,1)S(1)}, bf16[32,8,2048]{2,1,0:T(8,128)(2,1)S(1)}, bf16[32,8,2176]{2,1,0:T(8,128)(2,1)S(1)}) custom-call(bf16[64,32]{1,0:T(8,128)(2,1)S(1)} %get-tuple-element.57.refs_0_, bf16[64,32]{1,0:T(8,128)(2,1)S(1)} %get-tuple-element.59.refs_1_, bf16[32,2048]{1,0:T(8,128)(2,1)S(1)} %get-tuple-element.60.refs_2_, ...), custom_call_target="tpu_custom_call" | custom-call | tf_op jit(solution)/shard_map/dispatch_rows/pallas_call | solution.py:275
  129.3 22.1 %work_rows.3 = (bf16[16,8,2048]{2,1,0:T(8,128)(2,1)S(1)}, bf16[16,8,2048]{2,1,0:T(8,128)(2,1)S(1)}, bf16[16,8,128]{2,1,0:T(8,128)(2,1)S(1)}) custom-call(bf16[32,8,2048]{2,1,0:T(8,128)(2,1)S(1)} %get-tuple-element.21.refs_0_, bf16[32,8,2048]{2,1,0:T(8,128)(2,1)S(1)} %get-tuple-element.22.refs_1_, bf16[32,8,2176]{2,1,0:T(8,128)(2,1)S(1)} %get-tuple-element.23.refs_2_, ...), custom_call_target="tpu_custom_call" | custom-call | tf_op jit(solution)/shard_map/work_rows/pallas_call | solution.py:299
  151.6 0.7 copy-done.9
  152.5 0.4 fusion.5
  152.9 0.4 fusion.38
  153.4 0.4 fusion.4
  153.8 0.7 maximum_bitcast_fusion
  154.6 0.7 maximum_bitcast_fusion.1
  (81 shorter events, 2.0 us)
Async XLA Ops:
  0.6 5.4 %copy-start = (bf16[1,2048,8]{1,2,0:T(8,128)(2,1)S(1)}, bf16[1,2048,8]{1,2,0:T(8,128)(2,1)}, u32[]{:S(2)}) copy-start(bf16[1,2048,8]{1,2,0:T(8,128)(2,1)} %param.21) | copy-start | bytes 98308
  0.6 13.2 %copy-start.16 = (s32[2,2,1,32,2]{3,4,2,1,0:T(2,128)S(1)}, s32[2,2,1,32,2]{3,4,2,1,0:T(2,128)}, u32[]{:S(2)}) copy-start(s32[2,2,1,32,2]{3,4,2,1,0:T(2,128)} %param.18) | copy-start | bytes 3076
  0.7 8.9 %copy-start.13 = (f32[1,2048]{1,0:T(1,128)S(1)}, f32[1,2048]{1,0:T(1,128)}, u32[]{:S(2)}) copy-start(f32[1,2048]{1,0:T(1,128)} %param.20) | copy-start | bytes 24580
  0.7 10.7 %copy-start.23 = (s32[2,2,1,32]{3,2,1,0:T(1,128)S(1)}, s32[2,2,1,32]{3,2,1,0:T(1,128)}, u32[]{:S(2)}) copy-start(s32[2,2,1,32]{3,2,1,0:T(1,128)} %param.19) | copy-start | bytes 1540
  2.0 11.9 %copy-start.11 = (s32[2,2,1,32,2]{4,3,1,0,2:T(8,128)}, s32[2,2,1,32,2]{4,3,1,0,2:T(8,128)S(1)}, u32[]{:S(2)}) copy-start(s32[2,2,1,32,2]{4,3,1,0,2:T(8,128)S(1)} %copy.79) | copy-start | bytes 3076
  2.1 53.3 %copy-start.3 = (bf16[1,256,2048]{2,1,0:T(8,128)(2,1)S(1)}, bf16[1,256,2048]{2,1,0:T(8,128)(2,1)}, u32[]{:S(2)}) copy-start(bf16[1,256,2048]{2,1,0:T(8,128)(2,1)} %param.24) | copy-start | bytes 3145732
  6.0 6.2 %copy-start.17 = (f32[32]{0:T(128)}, f32[32]{0:T(128)S(1)}, u32[]{:S(2)}) copy-start(f32[32]{0:T(128)S(1)} %get-tuple-element.74) | copy-start | bytes 388
  7.7 47.7 %copy-start.2 = (bf16[1,2048,256]{2,1,0:T(8,128)(2,1)S(1)}, bf16[1,2048,256]{2,1,0:T(8,128)(2,1)}, u32[]{:S(2)}) copy-start(bf16[1,2048,256]{2,1,0:T(8,128)(2,1)} %param.23) | copy-start | bytes 3145732
  9.5 45.8 %copy-start.1 = (bf16[1,2048,256]{2,1,0:T(8,128)(2,1)S(1)}, bf16[1,2048,256]{2,1,0:T(8,128)(2,1)}, u32[]{:S(2)}) copy-start(bf16[1,2048,256]{2,1,0:T(8,128)(2,1)} %param.22) | copy-start | bytes 3145732
  18.1 63.6 %copy-start.8 = (f32[2,2,32,2,64]{4,2,3,1,0:T(8,128)}, f32[2,2,32,2,64]{4,2,3,1,0:T(8,128)S(1)}, u32[]{:S(2)}) copy-start(f32[2,2,32,2,64]{4,2,3,1,0:T(8,128)S(1)} %fusion.66) | copy-start | bytes 196612
  20.8 34.5 %copy-start.22 = (f32[128]{0:T(128)}, f32[128]{0:T(128)S(1)}, u32[]{:S(2)}) copy-start(f32[128]{0:T(128)S(1)} %compare_select_fusion.5) | copy-start | bytes 1540
  21.6 0.9 copy-start.4
  78.1 0.8 copy-start.12
  78.2 1.2 copy-start.6
  78.2 1.2 copy-start.18
  78.9 2.3 %copy-start.21 = (f32[32,8]{0,1:T(8,128)S(1)}, f32[32,8]{0,1:T(8,128)}, u32[]{:S(2)}) copy-start(f32[32,8]{0,1:T(8,128)} %fusion.57) | copy-start | bytes 3076
  78.9 3.3 %copy-start.10 = (bf16[1,32,2048]{2,1,0:T(8,128)(2,1)S(1)}, bf16[1,32,2048]{2,1,0:T(8,128)(2,1)}, u32[]{:S(2)}) copy-start(bf16[1,32,2048]{2,1,0:T(8,128)(2,1)} %param.13) | copy-start | bytes 393220
  79.4 12.7 %copy-start.5 = (bf16[1,32,2048]{2,1,0:T(8,128)(2,1)S(1)}, bf16[1,32,2048]{2,1,0:T(8,128)(2,1)}, u32[]{:S(2)}) copy-start(bf16[1,32,2048]{2,1,0:T(8,128)(2,1)} %param.16) | copy-start | bytes 393220
  81.0 0.6 copy-start.19
  82.6 8.4 %collective-permute-start = (bf16[32,2048]{1,0:T(8,128)(2,1)S(1)}, bf16[32,2048]{1,0:T(8,128)(2,1)}, u32[]{:S(2)}, u32[]{:S(2)}) collective-permute-start(bf16[32,2048]{1,0:T(8,128)(2,1)S(1)} %fusion.2), channel_id=1, source_target_pairs={{0,32},{32,64},{64,96},{96,128},{128,160},{160,192},{192,224},{224... | collective-permute-start | bytes 393224 | tf_op jit(solution)/shard_map/ppermute | solution.py:18
  90.3 8.9 %copy-start.14 = (bf16[1,32,2048]{2,1,0:T(8,128)(2,1)S(1)}, bf16[1,32,2048]{2,1,0:T(8,128)(2,1)}, u32[]{:S(2)}) copy-start(bf16[1,32,2048]{2,1,0:T(8,128)(2,1)} %param.17) | copy-start | bytes 393220
  93.5 5.7 %collective-permute-start.1 = (bf16[32,2048]{1,0:T(8,128)(2,1)S(1)}, bf16[32,2048]{1,0:T(8,128)(2,1)S(1)}, u32[]{:S(2)}, u32[]{:S(2)}) collective-permute-start(bf16[32,2048]{1,0:T(8,128)(2,1)S(1)} %get-tuple-element.54), channel_id=1, source_target_pairs={{32,0},{64,32},{96,64},{128,96},{160,128},{192,160},{224,192},{256... | collective-permute-start | bytes 393224 | tf_op jit(solution)/shard_map/ppermute | solution.py:18
  151.4 0.9 copy-start.9
  151.4 1.1 copy-start.15
  151.5 1.4 copy-start.7
  151.5 1.4 copy-start.20
